TPU v7x, 512 devices: a whole 4x4x16 slice. The times are simulated.
512 devices in a mesh: seq: 64 (over x, z), head: 8 (over y, core).
Axes of the slice: x: 4, y: 4, z: 16, core: 2. Of those that a mesh axis runs over, the one named last changes fastest.
Arguments:
- tokens: bfloat16 [32768, 1024], P(('seq', 'head')), may hold values from -6 to 6
- w_query: bfloat16 [1024, 1024], P(None, 'head'), may hold values from -0.1875 to 0.1875
- w_key: bfloat16 [1024, 1024], P(None, 'head'), may hold values from -0.1875 to 0.1875
- w_value: bfloat16 [1024, 1024], P(None, 'head'), may hold values from -0.1875 to 0.1875
- w_beta: bfloat16 [1024, 8], P(None, 'head'), may hold values from -0.09375 to 0.09375
- beta_bias: float32 [8], P('head'), may hold values from -1 to 3, as said below
- conv_weight: float32 [3, 4, 1024], P(None, None, 'head'), may hold values from -3 to 3
- norm_gain: float32 [1024], P('head'), may hold values from 0.1 to 1.9
- w_out: bfloat16 [1024, 1024], P('head'), may hold values from -0.1875 to 0.1875
Outputs:
- mixed: bfloat16 [32768, 1024], P(('seq', 'head'))
Inputs may be any that keep to these rules, and one draw needn't show every extreme that they name: `beta_bias`: one logit offset per head.
All inputs are finite; a program needn't handle non-finite values.
Results may differ from a plain program's by a relative error of at most 0.015.
The roundings to bfloat16 on the way count: a program that leaves them out, or rounds other values in their place, can miss the bound.
Values may be sent and summed in bfloat16 or wider, within the bound.
A program may use at most 64 MiB of HBM per device.

v0:
```python
import jax
import jax.numpy as jnp
from jax import lax
from jax.sharding import PartitionSpec as P

SPAN = 64


precise = lax.Precision.HIGHEST


def from_behind(shard, axis, by):
    length = lax.axis_size(axis)
    pairs = [(i, i + by) for i in range(length) if 0 <= i + by < length]
    return lax.ppermute(shard, axis, pairs)


def entering_2(shard, axis, combine, identity):
    length, position = (lax.axis_size(axis), lax.axis_index(axis))
    everything = jax.tree.map(lambda part: lax.all_gather(part, axis), shard)
    start = jax.tree.map(
        lambda part, zero: jnp.broadcast_to(jnp.asarray(zero, part.dtype), part.shape),
        shard,
        identity,
    )

    def lap(k, before):
        reached = k < position
        new = combine(before, jax.tree.map(lambda part: part[k], everything))
        return jax.tree.map(lambda a, b: jnp.where(reached, a, b), new, before)

    return lax.fori_loop(0, length, lap, start)


def compose(earlier_pair, later_pair):
    first_part = jnp.einsum("hij,hjk->hik", earlier_pair[0], later_pair[0], precision=precise)
    second = (
        jnp.einsum("hij,hjk->hik", earlier_pair[1], later_pair[0], precision=precise)
        + later_pair[1]
    )
    return (first_part, second)


def absorb(pair_sofar, block_in):
    return (compose(pair_sofar, block_in), None)


def local(tokens, w_query, w_key, w_value, w_beta, beta_bias, conv_weight, norm_gain, w_out):
    gathered = lax.all_gather(tokens, "head", axis=0, tiled=True)
    length = gathered.shape[0]
    heads_here = beta_bias.shape[0]
    head_width = w_query.shape[1]
    head_dim = head_width // heads_here
    tap_count = conv_weight.shape[1]
    joined = jnp.concatenate([w_query, w_key, w_value], 1)
    projected = jnp.dot(gathered, joined, preferred_element_type=jnp.float32).astype(jnp.bfloat16)
    logits = jnp.dot(gathered, w_beta, preferred_element_type=jnp.float32) + beta_bias
    beta_rate = 2.0 * jax.nn.sigmoid(logits)
    earlier = from_behind(projected[length - (tap_count - 1) :], "seq", 1)
    padded = jnp.concatenate([earlier, projected], 0).astype(jnp.float32)
    taps_weight = jnp.transpose(conv_weight, (1, 0, 2)).reshape(tap_count, 3 * head_width)
    mixed_conv = padded[0:length] * taps_weight[0]
    for offset in range(1, tap_count):
        mixed_conv = mixed_conv + padded[offset : offset + length] * taps_weight[offset]
    activated = jax.nn.silu(mixed_conv).astype(jnp.bfloat16)
    blocks = length // SPAN

    def arrange(columns_in):
        shaped = columns_in.reshape(blocks, SPAN, heads_here, head_dim)
        return jnp.transpose(shaped, (0, 2, 1, 3)).astype(jnp.float32)

    queries = arrange(activated[:, :head_width])
    keys_raw = arrange(activated[:, head_width : 2 * head_width])
    values_in = arrange(activated[:, 2 * head_width :])
    keys_unit = keys_raw / jnp.sqrt(jnp.sum(keys_raw * keys_raw, -1, keepdims=True) + 1e-06)
    block_rates = jnp.transpose(beta_rate.reshape(blocks, SPAN, heads_here), (0, 2, 1))
    key_gram = jnp.einsum("nhcd,nhed->nhce", keys_unit, keys_unit, precision=precise)
    query_gram = jnp.einsum("nhcd,nhed->nhce", queries, keys_unit, precision=precise)
    row_index = lax.broadcasted_iota(jnp.int32, (SPAN, SPAN), 0)
    col_index = lax.broadcasted_iota(jnp.int32, (SPAN, SPAN), 1)
    strict_lower = (row_index > col_index).astype(jnp.float32)
    lower_incl = (row_index >= col_index).astype(jnp.float32)
    system = jnp.eye(SPAN, dtype=jnp.float32) + block_rates[..., :, None] * key_gram * strict_lower
    right_sides = block_rates[..., None] * jnp.concatenate([keys_unit, values_in], -1)
    solved = lax.linalg.triangular_solve(
        system, right_sides, left_side=True, lower=True, unit_diagonal=True
    )
    weights_k = solved[..., :head_dim]
    fresh_values = solved[..., head_dim:]
    transit = jnp.eye(head_dim, dtype=jnp.float32) - jnp.einsum(
        "nhca,nhcb->nhab", weights_k, keys_unit, precision=precise
    )
    landed = jnp.einsum("nhcv,nhcb->nhvb", fresh_values, keys_unit, precision=precise)
    eye_heads = jnp.broadcast_to(
        jnp.eye(head_dim, dtype=jnp.float32), (heads_here, head_dim, head_dim)
    )
    empty_state = jnp.zeros((heads_here, head_dim, head_dim), jnp.float32)
    shard_pair = lax.scan(absorb, (eye_heads, empty_state), (transit, landed))[0]
    entering = entering_2(shard_pair, "seq", compose, (eye_heads, empty_state))[1]

    def emit_block(carried, block_in):
        query_b, key_b, weight_b, fresh_b, qgram_b = block_in
        update = fresh_b - jnp.einsum("hca,hva->hcv", weight_b, carried, precision=precise)
        output = jnp.einsum("hca,hva->hcv", query_b, carried, precision=precise)
        output = output + jnp.einsum(
            "hce,hev->hcv", qgram_b * lower_incl, update, precision=precise
        )
        carried = carried + jnp.einsum("hcv,hcb->hvb", update, key_b, precision=precise)
        return (carried, output)

    outputs = lax.scan(
        emit_block, entering, (queries, keys_unit, weights_k, fresh_values, query_gram)
    )[1]
    ordered = jnp.transpose(outputs, (0, 2, 1, 3)).reshape(length, heads_here, head_dim)
    gain_rows = norm_gain.reshape(heads_here, head_dim)
    scaled = ordered * lax.rsqrt(jnp.mean(ordered * ordered, -1, keepdims=True) + 1e-05) * gain_rows
    normed = scaled.astype(jnp.bfloat16).reshape(length, head_width)
    product = jnp.dot(normed, w_out, preferred_element_type=jnp.float32)
    return lax.psum_scatter(
        lax.optimization_barrier(product.astype(jnp.bfloat16))
        .astype(jnp.float32)
        .astype(jnp.bfloat16),
        "head",
        scatter_dimension=0,
        tiled=True,
    )


def solution(mesh):
    in_specs = (
        P(("seq", "head"), None),
        P(None, "head"),
        P(None, "head"),
        P(None, "head"),
        P(None, "head"),
        P("head"),
        P(None, None, "head"),
        P("head"),
        P("head", None),
    )
    out_specs = P(("seq", "head"), None)
    return jax.shard_map(local, mesh=mesh, in_specs=in_specs, out_specs=out_specs, check_vma=False)
```

profile of v0, /device:TPU:2, one launch (start us, length us, event | category | flops | bytes accessed | tf_op | source)
XLA Modules:
  0.0 583.5 jit_solution(9084837354674469325)
XLA Ops:
  9.0 35.9 %all-gather.6.cloned.1.call-done = bf16[512,1024]{1,0:T(8,128)(2,1)} async-done(((bf16[64,1024]{1,0:T(8,128)(2,1)}), bf16[512,1024]{1,0:T(8,128)(2,1)}) %all-gather.6.cloned.1.call-update) | async-done | bytes 1048592 | tf_op jit(solution)/shard_map/all_gather | solution.py:49
  44.9 2.2 fusion.43
  47.2 3.5 collective-permute-start
  51.1 5.2 collective-permute-done
  58.5 39.3 %custom-call.3 = f32[8,1,1,64,64]{3,4,2,1,0:T(8,128)S(1)} custom-call(f32[8,1,1,64,64]{4,3,2,1,0:T(8,128)S(1)} %fusion.48), custom_call_target="InvertDiagBlocksLowerTriangular" | custom-call | tf_op jit(solution)/shard_map/triangular_solve | solution.py:85
  100.8 6.1 %while.39 = (s32[]{:T(128)}, f32[1,128,128]{1,2,0:T(8,128)S(1)}, f32[1,128,128]{1,2,0:T(8,128)S(1)}, f32[8,1,128,128]{3,2,1,0:T(8,128)S(1)}, f32[8,1,128,128]{3,2,0,1:T(8,128)S(1)}, /*index=5*/s32[]{:T(128)}) while((s32[]{:T(128)}, f32[1,128,128]{1,2,0:T(8,128)S(1)}, f32[1,128,128]{1,2,0:T(8,128)S(1)}, f32[8,1,128,128]{3,2,1,0:T(8,128)S(1)}, ...), condition=%wide.region_2.3_spmd, body=%wide.region_1.2_spmd.sunk | while | flops 50348032 | bytes 983121 | solution.py:98
  109.3 142.0 %all-gather.8.cloned.1.call-done = f32[64,128,128]{2,1,0:T(8,128)} async-done(((f32[1,128,128]{2,1,0:T(8,128)}), f32[64,128,128]{2,1,0:T(8,128)}) %all-gather.8.cloned.1.call-update) | async-done | bytes 4194320 | tf_op jit(solution)/shard_map/all_gather | solution.py:20
  251.3 144.0 %all-gather.10.cloned.1.call-done = f32[64,128,128]{2,1,0:T(8,128)} async-done(((f32[1,128,128]{2,1,0:T(8,128)}), f32[64,128,128]{2,1,0:T(8,128)}) %all-gather.10.cloned.1.call-update) | async-done | bytes 4194320 | tf_op jit(solution)/shard_map/all_gather | solution.py:20
  395.4 135.6 %while.41 = (s32[]{:T(128)}, f32[1,128,128]{1,2,0:T(8,128)S(1)}, s32[]{:T(128)}, f32[64,1,128,128]{3,2,1,0:T(8,128)}, f32[64,1,128,128]{3,2,0,1:T(8,128)}, /*index=5*/s32[]{:T(128)}, s32[]{:T(128)}) while((s32[]{:T(128)}, f32[1,128,128]{1,2,0:T(8,128)S(1)}, s32[]{:T(128)}, f32[64,1,128,128]{3,2,1,0:T(8,128)}, ...), condition=%wide.region_4.5_spmd.clone, body=%wide.region_3.4_spmd.clone.sunk | while | flops 25231364 | bytes 723043 | solution.py:32
  398.4 1.1 fusion.126
  400.6 1.1 fusion.126
  402.7 1.1 fusion.126
  404.8 1.1 fusion.126
  406.9 1.1 fusion.126
  409.0 1.1 fusion.126
  411.1 1.1 fusion.126
  413.3 1.1 fusion.126
  417.5 1.1 fusion.126
  419.6 1.1 fusion.126
  421.7 1.1 fusion.126
  423.9 1.1 fusion.126
  426.0 1.1 fusion.126
  428.1 1.1 fusion.126
  430.2 1.1 fusion.126
  432.3 1.1 fusion.126
  436.6 1.1 fusion.126
  438.7 1.1 fusion.126
  440.8 1.1 fusion.126
  442.9 1.1 fusion.126
  445.0 1.1 fusion.126
  447.2 1.1 fusion.126
  449.3 1.1 fusion.126
  451.4 1.1 fusion.126
  455.6 1.1 fusion.126
  457.7 1.1 fusion.126
  459.9 1.1 fusion.126
  462.0 1.1 fusion.126
  464.1 1.1 fusion.126
  466.2 1.1 fusion.126
  468.3 1.1 fusion.126
  470.5 1.1 fusion.126
  474.7 1.1 fusion.126
  476.8 1.1 fusion.126
  478.9 1.1 fusion.126
  481.1 1.1 fusion.126
  483.2 1.1 fusion.126
  485.3 1.1 fusion.126
  487.4 1.1 fusion.126
  489.5 1.1 fusion.126
  493.8 1.1 fusion.126
  495.9 1.1 fusion.126
  498.0 1.1 fusion.126
  500.1 1.1 fusion.126
  502.2 1.1 fusion.126
  504.4 1.1 fusion.126
  506.5 1.1 fusion.126
  508.6 1.1 fusion.126
  512.8 1.1 fusion.126
  514.9 1.1 fusion.126
  517.1 1.1 fusion.126
  519.2 1.1 fusion.126
  531.0 7.9 %while.40 = (s32[]{:T(128)}, f32[1,128,128]{2,1,0:T(8,128)S(1)}, f32[8,1,64,128]{3,2,1,0:T(8,128)S(1)}, f32[8,1,64,128]{3,2,1,0:T(8,128)S(1)}, f32[8,1,64,128]{3...) while((s32[]{:T(128)}, f32[1,128,128]{2,1,0:T(8,128)S(1)}, ...), condition=%wide.region_6.7_spmd.clone, body=%wide.region_5.6_spmd.clone.sunk | while | flops 44085248 | bytes 624741 | solution.py:111
  539.3 1.4 convolution_convert_fusion
  540.7 36.3 %reduce-scatter.2.cloned.1.call-done = bf16[64,1024]{1,0:T(8,128)(2,1)} async-done(((bf16[512,1024]{1,0:T(8,128)(2,1)}), bf16[64,1024]{1,0:T(8,128)(2,1)}) %reduce-scatter.2.cloned.1.call-update) | async-done | bytes 131088 | tf_op jit(solution)/shard_map/reduce_scatter | solution.py:119
  (338 shorter events, 97.2 us)
Async XLA Ops:
  6.5 532.8 %copy-start = (bf16[128,1024]{1,0:T(8,128)(2,1)S(1)}, bf16[128,1024]{1,0:T(8,128)(2,1)}, u32[]{:S(2)}) copy-start(bf16[128,1024]{1,0:T(8,128)(2,1)} %param.23) | copy-start | bytes 786436
  6.5 38.4 %all-gather.6.cloned.1.call-start = ((), (), s32[]{:S(2)}) async-start(), calls=%async_computation.1 | async-start | bytes 1179648 | tf_op jit(solution)/shard_map/all_gather | solution.py:49
  7.3 244.1 %all-gather.8.cloned.1.call-start = ((), (), s32[]{:S(2)}) async-start(), calls=%async_computation.3 | async-start | bytes 4259840 | tf_op jit(solution)/shard_map/all_gather | solution.py:20
  8.9 41.8 %copy-start.2 = (bf16[1024,1]{0,1:T(2,128)(2,1)S(1)}, bf16[1024,1]{0,1:T(2,128)(2,1)}, u32[]{:S(2)}) copy-start(bf16[1024,1]{0,1:T(2,128)(2,1)} %param.19) | copy-start | bytes 6148
  44.9 5.8 copy-start.1
  47.2 9.1 %collective-permute-start = (bf16[3,384]{0,1:T(8,128)(2,1)S(1)}, bf16[3,384]{0,1:T(8,128)(2,1)S(1)}, u32[]{:S(2)}, u32[]{:S(2)}) collective-permute-start(bf16[3,384]{0,1:T(8,128)(2,1)S(1)} %slice.64), channel_id=1, source_target_pairs={{0,8},{8,16},{16,24},{24,32},{32,40},{40,48},{48,56},{56,64},{64,7... | collective-permute-start | bytes 6920 | tf_op jit(solution)/shard_map/ppermute | solution.py:15
  107.7 287.7 %all-gather.10.cloned.1.call-start = ((), (), s32[]{:S(2)}) async-start(), calls=%async_computation.4 | async-start | bytes 4259840 | tf_op jit(solution)/shard_map/all_gather | solution.py:20
  108.5 468.5 %reduce-scatter.2.cloned.1.call-start = ((), (), s32[]{:S(2)}) async-start(), calls=%async_computation.2 | async-start | bytes 1179648 | tf_op jit(solution)/shard_map/reduce_scatter | solution.py:119
  530.9 8.2 %copy-start.3 = (f32[128]{0:T(128)S(1)}, f32[128]{0:T(128)}, u32[]{:S(2)}) copy-start(f32[128]{0:T(128)} %param.22) | copy-start | bytes 1540
Sparse Core Ops, SparseCore 0:
  9.5 35.3 all-gather.5
  107.8 143.5 all-gather.7
  254.3 141.0 all-gather.9
  540.8 36.1 reduce-scatter.1
where the time goes:
time: 590 us; the launch traced here: 584 us
  waiting for transfers between devices  364 us (62%)
  matrix products  92.1 us (16%)
  local copies, waits for them, and re-layouts  64.5 us (11%)
  other arithmetic  41.3 us (7%)
  between operations  14.1 us (2%)
    all_gather x2, waiting for transfers between devices, entering_2(): everything = jax.tree.map(lambda part: lax.all_gather(part, axis), shard)  286 us
    dot_general x72, matrix products, compose(): jnp.einsum('hij,hjk->hik', earlier_pair[1], later_pair[0], precision=prec...  74.7 us
    dynamic_slice x128, local copies, waits for them, and re-layouts, lap(): new = combine(before, jax.tree.map(lambda part: part[k], everything))  59.9 us
    another operation x3, other arithmetic, local(): lax.linalg.triangular_solve(system, right_sides, left_side=True, lower=Tr...  39.4 us
    reduce_scatter x1, waiting for transfers between devices, local(): lax.psum_scatter(lax.optimization_barrier(product.astype(jnp.bfloat16)).a...  36.3 us
    all_gather x1, waiting for transfers between devices, local(): gathered = lax.all_gather(tokens, 'head', axis=0, tiled=True)  35.9 us
  transfers between devices with their start and end apart: 5, of which 5 were waited for; matrix products, arithmetic and copies ran while one was open for 1% of the time, Pallas kernels for 0%

commit v1 on v0

v1 whole, which is shorter than its diff:
```python
import functools

import jax
import jax.numpy as jnp
from jax import lax
from jax.experimental import pallas as pl
from jax.experimental.pallas import tpu as pltpu
from jax.sharding import PartitionSpec as P

F32, BF16 = jnp.float32, jnp.bfloat16
MESH = pl.DeviceIdType.MESH
Z_CHIPS = 16
Y_CHIPS = 4
D = 1024
HD = 128
ROWS = 64
SHARD = 512
CHUNK = 128
CHUNKS = SHARD // CHUNK
HALF = 32
HALO = 8

NN = (((1,), (0,)), ((), ()))
NT = (((1,), (1,)), ((), ()))
TN = (((0,), (0,)), ((), ()))


def dot(a, b, dims=NN):
    return lax.dot_general(a, b, dims, preferred_element_type=F32)


def split(a):
    high = a.astype(BF16)
    return high, (a - high.astype(F32)).astype(BF16)


def mm3(a, b):
    ah, al = split(a)
    bh, bl = split(b)
    return dot(ah, bh) + (dot(ah, bl) + dot(al, bh))


def after(earlier, later):
    return mm3(earlier, later[:HD]) + pad_top(later[HD:])


def pad_top(state):
    return jnp.concatenate([jnp.zeros((HD, HD), F32), state], 0)


def prepend(raw, acc):
    high, low = split(acc[:HD])
    return dot(raw, high) + dot(raw, low) + pad_top(acc[HD:])


def append(acc, raw):
    high, low = split(acc)
    step = raw[:HD]
    return dot(high, step) + dot(low, step) + pad_top(raw[HD:].astype(F32))


def invert(lowers):
    row = lax.broadcasted_iota(jnp.int32, (CHUNK, CHUNK), 0)
    col = lax.broadcasted_iota(jnp.int32, (CHUNK, CHUNK), 1)

    def pick(low, bits):
        r, c = lax.shift_right_logical(row, bits), lax.shift_right_logical(col, bits)
        mask = (lax.bitwise_and(r, 1) == 1) & (c == r - 1)
        return jnp.where(mask, low, 0.0)

    eye = (row == col).astype(F32)
    inverses = [eye - pick(low, 0) for low in lowers]
    bits = 1
    while (1 << bits) < CHUNK:
        first = [mm3(x, pick(low, bits)) for x, low in zip(inverses, lowers)]
        inverses = [x - mm3(f, x) for x, f in zip(inverses, first)]
        bits += 1
    return inverses


def layer(
    x_chips, z_chips,
    tok, wq, wk, wv, wb, bias, conv, gain, wo,
    out,
    gathered, halo, weights, outw, padded, logits,
    q_eff, o_loc, ring, lines, left, right, total_f, entering,
    give, got,
    load_sem, tok_send, tok_recv, halo_send, halo_recv, w_send, w_recv,
    ring_send, ring_recv, line_send, line_recv, give_send, got_recv,
):
    s, h = lax.axis_index("seq"), lax.axis_index("head")
    shards = x_chips * z_chips
    y, c = h // 2, h % 2
    x, z = s // z_chips, s % z_chips
    up, down, far = (y + 1) % Y_CHIPS, (y + 3) % Y_CHIPS, (y + 2) % Y_CHIPS
    other = 1 - c
    z_up, z_down = (z + 1) % z_chips, (z + z_chips - 1) % z_chips

    def head_of(yy, cc):
        return yy * 2 + cc

    partner = (s, head_of(y, other))

    def remote(src, dst, send, recv, device):
        return pltpu.make_async_remote_copy(
            src_ref=src, dst_ref=dst, send_sem=send, recv_sem=recv,
            device_id=device, device_id_type=MESH,
        )

    def arrived(dst, recv):
        remote(dst, dst, recv, recv, partner).wait_recv()

    loads = [
        pltpu.make_async_copy(w, weights.at[:, pl.ds(i * HD, HD)], load_sem.at[i])
        for i, w in enumerate((wq, wk, wv))
    ]
    own_wo = pltpu.make_async_copy(wo, outw.at[h], load_sem.at[3])
    own_tok = [
        pltpu.make_async_copy(
            tok.at[pl.ds(i * HALF, HALF)], gathered.at[y, c, i], load_sem.at[4 + i]
        )
        for i in range(2)
    ]
    for copy in (*own_tok, *loads, own_wo):
        copy.start()

    barrier = pltpu.get_barrier_semaphore()

    def greet(device):
        pl.semaphore_signal(barrier, inc=1, device_id=device, device_id_type=MESH)

    for step in range(1, 8):
        greet((s, (h + step) % 8))
    greet((x * z_chips + z_up, h))
    greet((x * z_chips + z_down, h))
    for step in range(1, x_chips):
        greet((((x + step) % x_chips) * z_chips + z, h))

    @pl.when(s > 0)
    def _():
        greet((s - 1, 7))

    sends_halo = (h == 7) & (s < shards - 1)

    @pl.when(sends_halo)
    def _():
        for peer in range(8):
            greet((s + 1, peer))

    pl.semaphore_wait(
        barrier,
        9 + (x_chips - 1) + jnp.where(s > 0, 1, 0) + jnp.where(sends_halo, 8, 0),
    )

    sent = []

    def tok_copy(src, yy, cc, half, device):
        copy = remote(
            src, gathered.at[yy, cc, half],
            tok_send.at[len(sent)], tok_recv.at[yy, cc, half], device,
        )
        copy.start()
        sent.append(copy)

    def relay(yy, half, device):
        tok_copy(gathered.at[yy, c, half], yy, c, half, device)

    to_up, to_down = (s, head_of(up, c)), (s, head_of(down, c))
    own = [tok.at[pl.ds(i * HALF, HALF)] for i in range(2)]
    tok_copy(own[0], y, c, 0, to_up)
    tok_copy(own[1], y, c, 1, to_down)
    tok_copy(own[1], y, c, 1, to_up)
    tok_copy(own[0], y, c, 0, to_down)
    tok_copy(own[0], y, c, 0, partner)
    tok_copy(own[1], y, c, 1, partner)

    def halo_copy(peer):
        return remote(
            tok.at[pl.ds(ROWS - HALO, HALO)], halo, halo_send.at[peer], halo_recv, (s + 1, peer)
        )

    @pl.when(sends_halo)
    def _():
        for peer in range(8):
            halo_copy(peer).start()

    @pl.when(s == 0)
    def _():
        halo[...] = jnp.zeros_like(halo)

    rate_rows = jnp.broadcast_to(wb[...].astype(F32), (HD, D))
    weights[:, pl.ds(3 * HD, HD)] = jnp.transpose(rate_rows).astype(BF16)
    for copy in loads:
        copy.wait()

    def project(yy):
        block = gathered[yy].reshape(CHUNK, D)
        result = dot(block, weights[...])
        start = pl.multiple_of(yy * CHUNK, CHUNK)
        padded[pl.ds(start + HALO, CHUNK), :] = result[:, : 3 * HD].astype(BF16).astype(F32)
        logits[pl.ds(start, CHUNK), :] = result[:, 3 * HD :]

    def tok_arrived(yy, cc, half):
        arrived(gathered.at[yy, cc, half], tok_recv.at[yy, cc, half])

    tok_arrived(down, c, 0)
    relay(down, 0, to_up)
    relay(down, 0, partner)
    tok_arrived(up, c, 1)
    relay(up, 1, to_down)
    relay(up, 1, partner)
    for half in range(2):
        own_tok[half].wait()
        tok_arrived(y, other, half)
    project(y)
    tok_arrived(down, c, 1)
    relay(down, 1, partner)
    tok_arrived(up, c, 0)
    relay(up, 0, partner)

    @pl.when(s > 0)
    def _():
        arrived(halo, halo_recv)

    edge = dot(halo[...], weights[...])[:, : 3 * HD].astype(BF16).astype(F32)
    padded[pl.ds(0, HALO), :] = edge
    for yy in (down, up):
        for half in range(2):
            tok_arrived(yy, other, half)
        project(yy)
    for half in range(2):
        tok_arrived(far, c, half)
        relay(far, half, partner)
    for half in range(2):
        tok_arrived(far, other, half)
    project(far)

    own_wo.wait()
    wo_sent = []

    def wo_copy(src, slot, device):
        copy = remote(src, outw.at[slot], w_send.at[len(wo_sent)], w_recv.at[slot], device)
        copy.start()
        wo_sent.append(copy)

    wo_copy(wo, h, to_up)
    wo_copy(wo, h, to_down)
    wo_copy(wo, h, (s, head_of(far, c)))
    wo_copy(wo, h, partner)

    row = lax.broadcasted_iota(jnp.int32, (CHUNK, CHUNK), 0)
    col = lax.broadcasted_iota(jnp.int32, (CHUNK, CHUNK), 1)
    parts, lowers, rights, attends = [], [], [], []
    for n in range(CHUNKS):
        base = n * CHUNK
        acts = []
        for i in range(3):
            lanes = pl.ds(i * HD, HD)
            total = padded[pl.ds(base + HALO - 3, CHUNK), lanes] * conv[i, 0:1]
            for j in range(1, 4):
                total = total + padded[pl.ds(base + HALO - 3 + j, CHUNK), lanes] * conv[i, j : j + 1]
            acts.append((total / (1.0 + jnp.exp(-total))).astype(BF16))
        query, key, value = acts
        key32 = key.astype(F32)
        inv = 1.0 / jnp.sqrt(jnp.sum(key32 * key32, -1, keepdims=True) + 1e-06)
        beta = 2.0 * jax.nn.sigmoid(logits[pl.ds(base, CHUNK), :] + bias[...])
        rate = beta * inv
        gram = dot(key, key, NT)
        lowers.append(jnp.where(row > col, (rate * inv) * gram, 0.0))
        rights.append(
            jnp.concatenate([(rate * inv) * key32, rate * value.astype(F32)], 1)
        )
        attends.append(jnp.where(row >= col, dot(query, key, NT), 0.0).astype(BF16))
        parts.append((query, key))
    inverses = invert(lowers)
    eye = (row == col).astype(F32)
    lead = jnp.concatenate([eye, jnp.zeros((HD, HD), F32)], 0)
    before = lead
    for n in range(CHUNKS):
        query, key = parts[n]
        solved = mm3(inverses[n], rights[n])
        high, low = split(solved)
        moved = dot(high, key, TN) + dot(low, key, TN)
        step = jnp.concatenate([eye - moved[:HD], moved[HD:]], 0)
        reach = dot(attends[n], high)
        eff = (query.astype(F32) - reach[:, :HD]).astype(BF16)
        if n == 0:
            q_eff[pl.ds(0, CHUNK), :] = eff
            o_loc[pl.ds(0, CHUNK), :] = reach[:, HD:]
            before = step
        else:
            turned = dot(eff, before.astype(BF16), NT)
            q_eff[pl.ds(n * CHUNK, CHUNK), :] = turned[:, :HD].astype(BF16)
            o_loc[pl.ds(n * CHUNK, CHUNK), :] = turned[:, HD:] + reach[:, HD:]
            before = after(before, step)
    total_f[...] = before

    ring[z] = before.astype(BF16)
    ring_sent = []

    def ring_copy(slot, device_z):
        copy = remote(
            ring.at[slot], ring.at[slot],
            ring_send.at[len(ring_sent)], ring_recv.at[slot], (x * z_chips + device_z, h),
        )
        copy.start()
        ring_sent.append(copy)

    ring_copy(z, z_up)
    if z_chips > 2:
        ring_copy(z, z_down)
    for i in range(2):
        left[i] = lead
        right[i] = lead
    reach_left, reach_right = z_chips // 2, z_chips // 2 - 1
    for k in range(1, reach_left + 1):
        slot = (z + z_chips - k) % z_chips
        arrived(ring.at[slot], ring_recv.at[slot])
        if k < reach_left:
            ring_copy(slot, z_up)
        slot_r = (z + k) % z_chips
        if k <= reach_right:
            arrived(ring.at[slot_r], ring_recv.at[slot_r])
            if k < reach_right:
                ring_copy(slot_r, z_down)
        side = jnp.where(k > z, 1, 0)
        left[side] = prepend(ring[slot], left[side])
        if k <= reach_right:
            side_r = jnp.where(z + k >= z_chips, 1, 0)
            right[side_r] = append(right[side_r], ring[slot_r])
    before = after(right[1], left[0])
    line = after(before, after(total_f[...], after(right[0], left[1])))

    lines[x] = line.astype(BF16)

    def line_copy(step):
        return remote(
            lines.at[x], lines.at[x], line_send.at[step - 1], line_recv.at[x],
            ((x + step) * z_chips + z, h),
        )

    for step in range(1, x_chips):

        @pl.when(x + step < x_chips)
        def _():
            line_copy(step).start()

    entering[...] = jnp.zeros_like(entering)
    for k in range(x_chips - 1):

        @pl.when(k < x)
        def _():
            arrived(lines.at[k], line_recv.at[k])
            entering[...] = mm_state(entering[...], lines[k])

    state = mm3(entering[...], before[:HD]) + before[HD:]

    for yy in (up, down, far):
        slot = head_of(yy, c)
        arrived(outw.at[slot], w_recv.at[slot])
        wo_copy(outw.at[slot], slot, partner)

    high, low = split(state)
    outputs = dot(q_eff[...], high, NT) + dot(q_eff[...], low, NT) + o_loc[...]
    scale = lax.rsqrt(jnp.mean(outputs * outputs, -1, keepdims=True) + 1e-05)
    normed = (outputs * scale * gain[...]).astype(BF16)
    for peer in range(8):
        give[peer] = normed[peer * ROWS : (peer + 1) * ROWS]
    handed = []
    for step in range(1, 8):
        peer = (h + step) % 8
        copy = remote(
            give.at[peer], got.at[h], give_send.at[step - 1], got_recv.at[h], (s, peer)
        )
        copy.start()
        handed.append(copy)
    got[h] = give[h]
    for yy in (y, up, down, far):
        slot = head_of(yy, other)
        arrived(outw.at[slot], w_recv.at[slot])
    for step in range(1, 8):
        peer = (h + step) % 8
        arrived(got.at[peer], got_recv.at[peer])
    mixed = jnp.zeros((ROWS, D), F32)
    for g in range(8):
        mixed = mixed + dot(got[g], outw[g]).astype(BF16).astype(F32)
    out[...] = mixed.astype(BF16)

    for copy in (*sent, *wo_sent, *ring_sent, *handed):
        copy.wait_send()
    for step in range(1, x_chips):

        @pl.when(x + step < x_chips)
        def _():
            line_copy(step).wait_send()

    @pl.when(sends_halo)
    def _():
        for peer in range(8):
            halo_copy(peer).wait_send()


def mm_state(state, raw):
    high, low = split(state)
    return dot(high, raw[:HD]) + dot(low, raw[:HD]) + raw[HD:].astype(F32)


def local(x_chips, z_chips, tokens, w_query, w_key, w_value, w_beta, beta_bias, conv_weight, norm_gain, w_out):
    anywhere = pl.BlockSpec(memory_space=pl.ANY)
    vmem = pl.BlockSpec(memory_space=pltpu.VMEM)
    dma = pltpu.SemaphoreType.DMA
    return pl.pallas_call(
        functools.partial(layer, x_chips, z_chips),
        out_shape=jax.ShapeDtypeStruct((ROWS, D), BF16),
        in_specs=[anywhere] * 4 + [vmem] * 4 + [anywhere],
        out_specs=vmem,
        scratch_shapes=[
            pltpu.VMEM((Y_CHIPS, 2, 2, HALF, D), BF16),
            pltpu.VMEM((HALO, D), BF16),
            pltpu.VMEM((D, 4 * HD), BF16),
            pltpu.VMEM((8, HD, D), BF16),
            pltpu.VMEM((HALO + SHARD, 3 * HD), F32),
            pltpu.VMEM((SHARD, HD), F32),
            pltpu.VMEM((SHARD, HD), BF16),
            pltpu.VMEM((SHARD, HD), F32),
            pltpu.VMEM((z_chips, 2 * HD, HD), BF16),
            pltpu.VMEM((x_chips, 2 * HD, HD), BF16),
            pltpu.VMEM((2, 2 * HD, HD), F32),
            pltpu.VMEM((2, 2 * HD, HD), F32),
            pltpu.VMEM((2 * HD, HD), F32),
            pltpu.VMEM((HD, HD), F32),
            pltpu.VMEM((8, ROWS, HD), BF16),
            pltpu.VMEM((8, ROWS, HD), BF16),
            dma((6,)),
            dma((14,)),
            dma((Y_CHIPS, 2, 2)),
            dma((8,)),
            dma,
            dma((7,)),
            dma((8,)),
            dma((z_chips,)),
            dma((z_chips,)),
            dma((x_chips,)),
            dma((x_chips,)),
            dma((7,)),
            dma((8,)),
        ],
        compiler_params=pltpu.CompilerParams(
            collective_id=0, has_side_effects=True, vmem_limit_bytes=48 * 1024 * 1024
        ),
    )(
        tokens, w_query, w_key, w_value,
        w_beta.reshape(1, D), beta_bias.reshape(1, 1), conv_weight,
        norm_gain.reshape(1, HD), w_out,
    )


def solution(mesh):
    z_chips = Z_CHIPS
    x_chips = mesh.shape["seq"] // z_chips
    in_specs = (
        P(("seq", "head"), None),
        P(None, "head"),
        P(None, "head"),
        P(None, "head"),
        P(None, "head"),
        P("head"),
        P(None, None, "head"),
        P("head"),
        P("head", None),
    )
    out_specs = P(("seq", "head"), None)
    return jax.shard_map(
        functools.partial(local, x_chips, z_chips),
        mesh=mesh, in_specs=in_specs, out_specs=out_specs, check_vma=False,
    )
```

time: 590 us -> 74.5 us (0.13)
  the two profiles are of different devices: /device:TPU:2 before, /device:TPU:7 now
where the time goes in v1:
time: 74.5 us; the launch traced here: 74.1 us
  Pallas kernels  66.8 us (90%)
  local copies, waits for them, and re-layouts  6.7 us (9%)
    pallas_call x1, Pallas kernels, local(): pl.pallas_call(functools.partial(layer, x_chips, z_chips), out_shape=jax....  66.8 us
    unnamed x17, local copies, waits for them, and re-layouts  6.7 us

profile of v1, /device:TPU:7, one launch (start us, length us, event | category | flops | bytes accessed | tf_op | source)
XLA Modules:
  0.0 74.1 jit_solution(11384694656338488272)
XLA Ops:
  0.0 0.0 copy-start.5
  0.7 0.0 copy-start.7
  0.7 0.0 copy-done.5
  0.7 0.6 copy-done.7
  1.3 0.0 copy-start
  1.3 0.9 %copy-done = bf16[1024,128]{1,0:T(8,128)(2,1)S(1)} copy-done((bf16[1024,128]{1,0:T(8,128)(2,1)S(1)}, bf16[1024,128]{1,0:T(8,128)(2,1)}, u32[]{:S(2)}) %copy-start) | copy-done | bytes 262168
  2.3 0.0 copy-start.1
  2.3 0.9 %copy-done.1 = bf16[1024,128]{1,0:T(8,128)(2,1)S(1)} copy-done((bf16[1024,128]{1,0:T(8,128)(2,1)S(1)}, bf16[1024,128]{1,0:T(8,128)(2,1)}, u32[]{:S(2)}) %copy-start.1) | copy-done | bytes 262168
  3.2 0.0 copy-start.2
  3.2 0.9 %copy-done.2 = bf16[1024,128]{1,0:T(8,128)(2,1)S(1)} copy-done((bf16[1024,128]{1,0:T(8,128)(2,1)S(1)}, bf16[1024,128]{1,0:T(8,128)(2,1)}, u32[]{:S(2)}) %copy-start.2) | copy-done | bytes 262168
  4.2 0.0 copy-start.3
  4.2 0.9 %copy-done.3 = bf16[128,1024]{1,0:T(8,128)(2,1)S(1)} copy-done((bf16[128,1024]{1,0:T(8,128)(2,1)S(1)}, bf16[128,1024]{1,0:T(8,128)(2,1)}, u32[]{:S(2)}) %copy-start.3) | copy-done | bytes 262168
  5.1 0.0 copy-start.4
  5.1 0.9 %copy-done.4 = bf16[64,1024]{1,0:T(8,128)(2,1)S(1)} copy-done((bf16[64,1024]{1,0:T(8,128)(2,1)S(1)}, bf16[64,1024]{1,0:T(8,128)(2,1)}, u32[]{:S(2)}) %copy-start.4) | copy-done | bytes 131096
  6.0 0.0 copy-start.6
  6.0 0.7 copy-done.6
  6.7 66.8 %shard_map.91 = bf16[64,1024]{1,0:T(8,128)(2,1)S(1)} custom-call(bf16[64,1024]{1,0:T(8,128)(2,1)S(1)} %copy-done.4, bf16[1024,128]{1,0:T(8,128)(2,1)S(1)} %copy-done, bf16[1024,128]{1,0:T(8,128)(2,1)S(1)} %copy-done.1, bf16[1024,128]{1,0:T(8,128)(2,1)S(1)} %copy-done.2, bf16[1,1024]{1,0:T(2,128)(2,1)S(1)} %bitcast.4, f32[1,1]{1,0:T(1,128)} %bitcast.3.bias, ...), custom_call_target="tpu_custom_call" | custom-call | tf_op jit(solution)/shard_map/pallas_call | solution.py:412
  73.5 0.7 copy.12
Async XLA Ops:
  0.0 0.7 copy-start.5
  0.7 0.7 copy-start.7
  1.3 0.9 %copy-start = (bf16[1024,128]{1,0:T(8,128)(2,1)S(1)}, bf16[1024,128]{1,0:T(8,128)(2,1)}, u32[]{:S(2)}) copy-start(bf16[1024,128]{1,0:T(8,128)(2,1)} %wq.1) | copy-start | bytes 786436
  2.3 0.9 %copy-start.1 = (bf16[1024,128]{1,0:T(8,128)(2,1)S(1)}, bf16[1024,128]{1,0:T(8,128)(2,1)}, u32[]{:S(2)}) copy-start(bf16[1024,128]{1,0:T(8,128)(2,1)} %wk.1) | copy-start | bytes 786436
  3.2 0.9 %copy-start.2 = (bf16[1024,128]{1,0:T(8,128)(2,1)S(1)}, bf16[1024,128]{1,0:T(8,128)(2,1)}, u32[]{:S(2)}) copy-start(bf16[1024,128]{1,0:T(8,128)(2,1)} %wv.1) | copy-start | bytes 786436
  4.2 0.9 %copy-start.3 = (bf16[128,1024]{1,0:T(8,128)(2,1)S(1)}, bf16[128,1024]{1,0:T(8,128)(2,1)}, u32[]{:S(2)}) copy-start(bf16[128,1024]{1,0:T(8,128)(2,1)} %wo.1) | copy-start | bytes 786436
  5.1 0.9 %copy-start.4 = (bf16[64,1024]{1,0:T(8,128)(2,1)S(1)}, bf16[64,1024]{1,0:T(8,128)(2,1)}, u32[]{:S(2)}) copy-start(bf16[64,1024]{1,0:T(8,128)(2,1)} %tok.1) | copy-start | bytes 393220
  6.0 0.7 copy-start.6

commit v2 on v1

--- a/solution.py
+++ b/solution.py
@@ -17,8 +17,9 @@
 SHARD = 512
 CHUNK = 128
 CHUNKS = SHARD // CHUNK
-HALF = 32
+PART = 16
 HALO = 8
+SUBS = 4
 
 NN = (((1,), (0,)), ((), ()))
 NT = (((1,), (1,)), ((), ()))
@@ -80,13 +81,14 @@
 
 def layer(
     x_chips, z_chips,
-    tok, wq, wk, wv, wb, bias, conv, gain, wo,
+    tok, wq, wk, wv, wb_in, bias_in, conv_in, gain_in, wo,
     out,
+    wb, bias, conv, gain,
     gathered, halo, weights, outw, padded, logits,
-    q_eff, o_loc, ring, lines, left, right, total_f, entering,
+    q_eff, o_loc, ring, lines, left, right, own_f, prefix, duo, entering,
     give, got,
     load_sem, tok_send, tok_recv, halo_send, halo_recv, w_send, w_recv,
-    ring_send, ring_recv, line_send, line_recv, give_send, got_recv,
+    duo_send, duo_recv, ring_send, ring_recv, line_send, line_recv, give_send, got_recv,
 ):
     s, h = lax.axis_index("seq"), lax.axis_index("head")
     shards = x_chips * z_chips
@@ -94,7 +96,6 @@
     x, z = s // z_chips, s % z_chips
     up, down, far = (y + 1) % Y_CHIPS, (y + 3) % Y_CHIPS, (y + 2) % Y_CHIPS
     other = 1 - c
-    z_up, z_down = (z + 1) % z_chips, (z + z_chips - 1) % z_chips
 
     def head_of(yy, cc):
         return yy * 2 + cc
@@ -115,13 +116,19 @@
         for i, w in enumerate((wq, wk, wv))
     ]
     own_wo = pltpu.make_async_copy(wo, outw.at[h], load_sem.at[3])
+    small = [
+        pltpu.make_async_copy(src, dst, load_sem.at[6 + i])
+        for i, (src, dst) in enumerate(
+            ((wb_in, wb), (bias_in, bias), (conv_in, conv), (gain_in, gain))
+        )
+    ]
     own_tok = [
         pltpu.make_async_copy(
-            tok.at[pl.ds(i * HALF, HALF)], gathered.at[y, c, i], load_sem.at[4 + i]
-        )
-        for i in range(2)
+            tok.at[pl.ds(i * PART, PART)], gathered.at[y, c, i], load_sem.at[10 + i]
+        )
+        for i in range(4)
     ]
-    for copy in (*own_tok, *loads, own_wo):
+    for copy in (*own_tok, *small, *loads, own_wo):
         copy.start()
 
     barrier = pltpu.get_barrier_semaphore()
@@ -131,8 +138,8 @@
 
     for step in range(1, 8):
         greet((s, (h + step) % 8))
-    greet((x * z_chips + z_up, h))
-    greet((x * z_chips + z_down, h))
+    for hops in (z + 1 - 2 * (z % 2), (z + 2) % z_chips, (z + z_chips - 2) % z_chips):
+        greet((x * z_chips + hops, h))
     for step in range(1, x_chips):
         greet((((x + step) % x_chips) * z_chips + z, h))
 
@@ -149,7 +156,7 @@
 
     pl.semaphore_wait(
         barrier,
-        9 + (x_chips - 1) + jnp.where(s > 0, 1, 0) + jnp.where(sends_halo, 8, 0),
+        10 + (x_chips - 1) + jnp.where(s > 0, 1, 0) + jnp.where(sends_halo, 8, 0),
     )
 
     sent = []
@@ -166,13 +173,14 @@
         tok_copy(gathered.at[yy, c, half], yy, c, half, device)
 
     to_up, to_down = (s, head_of(up, c)), (s, head_of(down, c))
-    own = [tok.at[pl.ds(i * HALF, HALF)] for i in range(2)]
-    tok_copy(own[0], y, c, 0, to_up)
-    tok_copy(own[1], y, c, 1, to_down)
-    tok_copy(own[1], y, c, 1, to_up)
-    tok_copy(own[0], y, c, 0, to_down)
-    tok_copy(own[0], y, c, 0, partner)
-    tok_copy(own[1], y, c, 1, partner)
+    for copy in own_tok:
+        copy.wait()
+    own = [gathered.at[y, c, i] for i in range(4)]
+    for first, second in ((0, 2), (1, 3), (2, 0), (3, 1)):
+        tok_copy(own[first], y, c, first, to_up)
+        tok_copy(own[second], y, c, second, to_down)
+    for i in range(4):
+        tok_copy(own[i], y, c, i, partner)
 
     def halo_copy(peer):
         return remote(
@@ -188,6 +196,8 @@
     def _():
         halo[...] = jnp.zeros_like(halo)
 
+    for copy in small:
+        copy.wait()
     rate_rows = jnp.broadcast_to(wb[...].astype(F32), (HD, D))
     weights[:, pl.ds(3 * HD, HD)] = jnp.transpose(rate_rows).astype(BF16)
     for copy in loads:
@@ -203,50 +213,80 @@
     def tok_arrived(yy, cc, half):
         arrived(gathered.at[yy, cc, half], tok_recv.at[yy, cc, half])
 
-    tok_arrived(down, c, 0)
-    relay(down, 0, to_up)
-    relay(down, 0, partner)
-    tok_arrived(up, c, 1)
-    relay(up, 1, to_down)
-    relay(up, 1, partner)
-    for half in range(2):
-        own_tok[half].wait()
-        tok_arrived(y, other, half)
+    def near_arrived(up_part, down_part, onward):
+        tok_arrived(down, c, up_part)
+        if onward:
+            relay(down, up_part, to_up)
+        relay(down, up_part, partner)
+        tok_arrived(up, c, down_part)
+        if onward:
+            relay(up, down_part, to_down)
+        relay(up, down_part, partner)
+
+    near_arrived(0, 2, True)
+    near_arrived(1, 3, True)
+    for part in range(4):
+        tok_arrived(y, other, part)
     project(y)
-    tok_arrived(down, c, 1)
-    relay(down, 1, partner)
-    tok_arrived(up, c, 0)
-    relay(up, 0, partner)
-
+    near_arrived(2, 0, False)
+    near_arrived(3, 1, False)
     @pl.when(s > 0)
     def _():
         arrived(halo, halo_recv)
 
     edge = dot(halo[...], weights[...])[:, : 3 * HD].astype(BF16).astype(F32)
     padded[pl.ds(0, HALO), :] = edge
+    for part in (0, 2, 1, 3):
+        tok_arrived(far, c, part)
+        relay(far, part, partner)
     for yy in (down, up):
-        for half in range(2):
-            tok_arrived(yy, other, half)
+        for part in range(4):
+            tok_arrived(yy, other, part)
         project(yy)
-    for half in range(2):
-        tok_arrived(far, c, half)
-        relay(far, half, partner)
-    for half in range(2):
-        tok_arrived(far, other, half)
+    for part in range(4):
+        tok_arrived(far, other, part)
     project(far)
 
     own_wo.wait()
     wo_sent = []
 
-    def wo_copy(src, slot, device):
-        copy = remote(src, outw.at[slot], w_send.at[len(wo_sent)], w_recv.at[slot], device)
+    def wo_copy(src, slot, half, device):
+        copy = remote(
+            src.at[pl.ds(half * ROWS, ROWS)], outw.at[slot, pl.ds(half * ROWS, ROWS)],
+            w_send.at[len(wo_sent)], w_recv.at[slot, half], device,
+        )
         copy.start()
         wo_sent.append(copy)
 
-    wo_copy(wo, h, to_up)
-    wo_copy(wo, h, to_down)
-    wo_copy(wo, h, (s, head_of(far, c)))
-    wo_copy(wo, h, partner)
+    def wo_relay(yy, half, device):
+        slot = head_of(yy, c)
+        wo_copy(outw.at[slot], slot, half, device)
+
+    def wo_arrived(yy, cc, half):
+        slot = head_of(yy, cc)
+        arrived(outw.at[slot, pl.ds(half * ROWS, ROWS)], w_recv.at[slot, half])
+
+    wo_copy(outw.at[h], h, 0, to_up)
+    wo_copy(outw.at[h], h, 1, to_down)
+    wo_copy(outw.at[h], h, 1, to_up)
+    wo_copy(outw.at[h], h, 0, to_down)
+    wo_copy(outw.at[h], h, 0, partner)
+    wo_copy(outw.at[h], h, 1, partner)
+
+    def wo_relay_near():
+        for yy, first, onward in ((down, 0, to_up), (up, 1, to_down)):
+            wo_arrived(yy, c, first)
+            wo_relay(yy, first, onward)
+        for yy in (down, up):
+            for half in range(2):
+                if (yy is down) == (half == 1):
+                    wo_arrived(yy, c, half)
+                wo_relay(yy, half, partner)
+
+    def wo_relay_far():
+        for half in range(2):
+            wo_arrived(far, c, half)
+            wo_relay(far, half, partner)
 
     row = lax.broadcasted_iota(jnp.int32, (CHUNK, CHUNK), 0)
     col = lax.broadcasted_iota(jnp.int32, (CHUNK, CHUNK), 1)
@@ -263,7 +303,7 @@
         query, key, value = acts
         key32 = key.astype(F32)
         inv = 1.0 / jnp.sqrt(jnp.sum(key32 * key32, -1, keepdims=True) + 1e-06)
-        beta = 2.0 * jax.nn.sigmoid(logits[pl.ds(base, CHUNK), :] + bias[...])
+        beta = 2.0 * jax.nn.sigmoid(logits[pl.ds(base, CHUNK), :] + bias[0])
         rate = beta * inv
         gram = dot(key, key, NT)
         lowers.append(jnp.where(row > col, (rate * inv) * gram, 0.0))
@@ -275,61 +315,107 @@
     inverses = invert(lowers)
     eye = (row == col).astype(F32)
     lead = jnp.concatenate([eye, jnp.zeros((HD, HD), F32)], 0)
-    before = lead
+    before, entry, reached = lead, [], []
     for n in range(CHUNKS):
         query, key = parts[n]
         solved = mm3(inverses[n], rights[n])
         high, low = split(solved)
         moved = dot(high, key, TN) + dot(low, key, TN)
         step = jnp.concatenate([eye - moved[:HD], moved[HD:]], 0)
-        reach = dot(attends[n], high)
-        eff = (query.astype(F32) - reach[:, :HD]).astype(BF16)
-        if n == 0:
-            q_eff[pl.ds(0, CHUNK), :] = eff
-            o_loc[pl.ds(0, CHUNK), :] = reach[:, HD:]
-            before = step
-        else:
-            turned = dot(eff, before.astype(BF16), NT)
-            q_eff[pl.ds(n * CHUNK, CHUNK), :] = turned[:, :HD].astype(BF16)
-            o_loc[pl.ds(n * CHUNK, CHUNK), :] = turned[:, HD:] + reach[:, HD:]
-            before = after(before, step)
-    total_f[...] = before
-
-    ring[z] = before.astype(BF16)
-    ring_sent = []
-
-    def ring_copy(slot, device_z):
-        copy = remote(
-            ring.at[slot], ring.at[slot],
-            ring_send.at[len(ring_sent)], ring_recv.at[slot], (x * z_chips + device_z, h),
-        )
-        copy.start()
-        ring_sent.append(copy)
-
-    ring_copy(z, z_up)
-    if z_chips > 2:
-        ring_copy(z, z_down)
+        entry.append(before)
+        reached.append(high)
+        before = step if n == 0 else after(before, step)
+
+    def finish_outputs():
+        for n in range(CHUNKS):
+            reach = dot(attends[n], reached[n])
+            eff = (parts[n][0].astype(F32) - reach[:, :HD]).astype(BF16)
+            if n == 0:
+                q_eff[pl.ds(0, CHUNK), :] = eff
+                o_loc[pl.ds(0, CHUNK), :] = reach[:, HD:]
+            else:
+                turned = dot(eff, entry[n].astype(BF16), NT)
+                q_eff[pl.ds(n * CHUNK, CHUNK), :] = turned[:, :HD].astype(BF16)
+                o_loc[pl.ds(n * CHUNK, CHUNK), :] = turned[:, HD:] + reach[:, HD:]
+
+
+    halves = z % 2
+    z_other = z + 1 - 2 * halves
+    duo[halves] = before.astype(BF16)
+    duo_copy = remote(
+        duo.at[halves], duo.at[halves], duo_send, duo_recv.at[halves], (x * z_chips + z_other, h)
+    )
+    duo_copy.start()
+    finish_outputs()
     for i in range(2):
         left[i] = lead
         right[i] = lead
-    reach_left, reach_right = z_chips // 2, z_chips // 2 - 1
+    arrived(duo.at[1 - halves], duo_recv.at[1 - halves])
+
+    @pl.when(halves == 0)
+    def _():
+        own_f[...] = append(before, duo[1])
+
+    @pl.when(halves == 1)
+    def _():
+        own_f[...] = prepend(duo[0], before)
+
+    pairs = z_chips // 2
+    j = z // 2
+    ring[j] = own_f[...].astype(BF16).reshape(SUBS, 2 * HD // SUBS, HD)
+    ring_sent = []
+    two_up = (x * z_chips + (z + 2) % z_chips, h)
+    two_down = (x * z_chips + (z + z_chips - 2) % z_chips, h)
+
+    def ring_copy(slot, q, device):
+        copy = remote(
+            ring.at[slot, q], ring.at[slot, q],
+            ring_send.at[len(ring_sent)], ring_recv.at[slot, q], device,
+        )
+        copy.start()
+        ring_sent.append(copy)
+
+    reach_left, reach_right = pairs // 2, (pairs - 1) // 2
+    for q in range(SUBS):
+        ring_copy(j, q, two_up)
+        if reach_right > 0:
+            ring_copy(j, q, two_down)
+
+    def compose(k):
+        slot = (j + pairs - k) % pairs
+        side = jnp.where(k > j, 1, 0)
+        left[side] = prepend(ring[slot].reshape(2 * HD, HD), left[side])
+        if k <= reach_right:
+            slot_r = (j + k) % pairs
+            side_r = jnp.where(j + k >= pairs, 1, 0)
+            right[side_r] = append(right[side_r], ring[slot_r].reshape(2 * HD, HD))
+
     for k in range(1, reach_left + 1):
-        slot = (z + z_chips - k) % z_chips
-        arrived(ring.at[slot], ring_recv.at[slot])
-        if k < reach_left:
-            ring_copy(slot, z_up)
-        slot_r = (z + k) % z_chips
-        if k <= reach_right:
-            arrived(ring.at[slot_r], ring_recv.at[slot_r])
-            if k < reach_right:
-                ring_copy(slot_r, z_down)
-        side = jnp.where(k > z, 1, 0)
-        left[side] = prepend(ring[slot], left[side])
-        if k <= reach_right:
-            side_r = jnp.where(z + k >= z_chips, 1, 0)
-            right[side_r] = append(right[side_r], ring[slot_r])
+        slot = (j + pairs - k) % pairs
+        slot_r = (j + k) % pairs
+        for q in range(SUBS):
+            arrived(ring.at[slot, q], ring_recv.at[slot, q])
+            if k < reach_left:
+                ring_copy(slot, q, two_up)
+            if k <= reach_right:
+                arrived(ring.at[slot_r, q], ring_recv.at[slot_r, q])
+                if k < reach_right:
+                    ring_copy(slot_r, q, two_down)
+        if k == 1:
+            wo_relay_near()
+        if k == max(1, reach_left - 1):
+            wo_relay_far()
+            for done in range(1, k + 1):
+                compose(done)
+    if reach_left > 1:
+        compose(reach_left)
     before = after(right[1], left[0])
-    line = after(before, after(total_f[...], after(right[0], left[1])))
+    line = after(before, after(own_f[...], after(right[0], left[1])))
+    prefix[...] = before
+
+    @pl.when(halves == 1)
+    def _():
+        prefix[...] = append(before, duo[0])
 
     lines[x] = line.astype(BF16)
 
@@ -353,12 +439,7 @@
             arrived(lines.at[k], line_recv.at[k])
             entering[...] = mm_state(entering[...], lines[k])
 
-    state = mm3(entering[...], before[:HD]) + before[HD:]
-
-    for yy in (up, down, far):
-        slot = head_of(yy, c)
-        arrived(outw.at[slot], w_recv.at[slot])
-        wo_copy(outw.at[slot], slot, partner)
+    state = mm3(entering[...], prefix[pl.ds(0, HD)]) + prefix[pl.ds(HD, HD)]
 
     high, low = split(state)
     outputs = dot(q_eff[...], high, NT) + dot(q_eff[...], low, NT) + o_loc[...]
@@ -376,8 +457,8 @@
         handed.append(copy)
     got[h] = give[h]
     for yy in (y, up, down, far):
-        slot = head_of(yy, other)
-        arrived(outw.at[slot], w_recv.at[slot])
+        for half in range(2):
+            wo_arrived(yy, other, half)
     for step in range(1, 8):
         peer = (h + step) % 8
         arrived(got.at[peer], got_recv.at[peer])
@@ -386,7 +467,7 @@
         mixed = mixed + dot(got[g], outw[g]).astype(BF16).astype(F32)
     out[...] = mixed.astype(BF16)
 
-    for copy in (*sent, *wo_sent, *ring_sent, *handed):
+    for copy in (*sent, *wo_sent, duo_copy, *ring_sent, *handed):
         copy.wait_send()
     for step in range(1, x_chips):
 
@@ -406,16 +487,20 @@
 
 
 def local(x_chips, z_chips, tokens, w_query, w_key, w_value, w_beta, beta_bias, conv_weight, norm_gain, w_out):
-    anywhere = pl.BlockSpec(memory_space=pl.ANY)
+    hbm = pl.BlockSpec(memory_space=pltpu.HBM)
     vmem = pl.BlockSpec(memory_space=pltpu.VMEM)
     dma = pltpu.SemaphoreType.DMA
     return pl.pallas_call(
         functools.partial(layer, x_chips, z_chips),
         out_shape=jax.ShapeDtypeStruct((ROWS, D), BF16),
-        in_specs=[anywhere] * 4 + [vmem] * 4 + [anywhere],
+        in_specs=[hbm] * 9,
         out_specs=vmem,
         scratch_shapes=[
-            pltpu.VMEM((Y_CHIPS, 2, 2, HALF, D), BF16),
+            pltpu.VMEM((1, D), BF16),
+            pltpu.SMEM((1,), F32),
+            pltpu.VMEM((3, 4, HD), F32),
+            pltpu.VMEM((1, HD), F32),
+            pltpu.VMEM((Y_CHIPS, 2, 4, PART, D), BF16),
             pltpu.VMEM((HALO, D), BF16),
             pltpu.VMEM((D, 4 * HD), BF16),
             pltpu.VMEM((8, HD, D), BF16),
@@ -423,34 +508,38 @@
             pltpu.VMEM((SHARD, HD), F32),
             pltpu.VMEM((SHARD, HD), BF16),
             pltpu.VMEM((SHARD, HD), F32),
-            pltpu.VMEM((z_chips, 2 * HD, HD), BF16),
+            pltpu.VMEM((z_chips // 2, SUBS, 2 * HD // SUBS, HD), BF16),
             pltpu.VMEM((x_chips, 2 * HD, HD), BF16),
             pltpu.VMEM((2, 2 * HD, HD), F32),
             pltpu.VMEM((2, 2 * HD, HD), F32),
             pltpu.VMEM((2 * HD, HD), F32),
+            pltpu.VMEM((2 * HD, HD), F32),
+            pltpu.VMEM((2, 2 * HD, HD), BF16),
             pltpu.VMEM((HD, HD), F32),
             pltpu.VMEM((8, ROWS, HD), BF16),
             pltpu.VMEM((8, ROWS, HD), BF16),
-            dma((6,)),
             dma((14,)),
-            dma((Y_CHIPS, 2, 2)),
+            dma((28,)),
+            dma((Y_CHIPS, 2, 4)),
             dma((8,)),
             dma,
-            dma((7,)),
-            dma((8,)),
-            dma((z_chips,)),
-            dma((z_chips,)),
+            dma((14,)),
+            dma((8, 2)),
+            dma,
+            dma((2,)),
+            dma((z_chips // 2 * SUBS,)),
+            dma((z_chips // 2, SUBS)),
             dma((x_chips,)),
             dma((x_chips,)),
             dma((7,)),
             dma((8,)),
         ],
         compiler_params=pltpu.CompilerParams(
-            collective_id=0, has_side_effects=True, vmem_limit_bytes=48 * 1024 * 1024
+            collective_id=0, has_side_effects=True, vmem_limit_bytes=67043328
         ),
     )(
         tokens, w_query, w_key, w_value,
-        w_beta.reshape(1, D), beta_bias.reshape(1, 1), conv_weight,
+        w_beta.reshape(1, D), beta_bias, conv_weight,
         norm_gain.reshape(1, HD), w_out,
     )
 

time: 74.5 us -> 63.4 us (0.85)
  the two profiles are of different devices: /device:TPU:7 before, /device:TPU:37 now
where the time goes in v2:
time: 63.4 us; the launch traced here: 63.2 us
  Pallas kernels  61 us (96%)
  local copies, waits for them, and re-layouts  1.57 us (2%)
  between operations  0.66 us (1%)
    pallas_call x1, Pallas kernels, local(): pl.pallas_call(functools.partial(layer, x_chips, z_chips), out_shape=jax....  61 us
    unnamed x1, local copies, waits for them, and re-layouts  1.57 us

profile of v2, /device:TPU:37, one launch (start us, length us, event | category | flops | bytes accessed | tf_op | source)
XLA Modules:
  0.0 63.2 jit_solution(10672232698724386114)
XLA Ops:
  0.7 61.0 %shard_map.91 = bf16[64,1024]{1,0:T(8,128)(2,1)} custom-call(bf16[64,1024]{1,0:T(8,128)(2,1)} %tok.1, bf16[1024,128]{1,0:T(8,128)(2,1)} %wq.1, bf16[1024,128]{1,0:T(8,128)(2,1)} %wk.1, bf16[1024,128]{1,0:T(8,128)(2,1)} %wv.1, bf16[1,1024]{1,0:T(2,128)(2,1)} %bitcast.2, f32[1]{0:T(128)S(6)} %copy.11.bias_in, f32[3,4,128]{2,1,0:T(4,128)} %conv_in.1, ...), custom_call_target="tpu_custom_call" | custom-call | tf_op jit(solution)/shard_map/pallas_call | solution.py:493
  61.7 1.6 %copy.12 = bf16[64,1024]{1,0:T(8,128)(2,1)} copy(bf16[64,1024]{1,0:T(8,128)(2,1)} %shard_map.91) | data formatting | bytes 262144

commit v3 on v2

--- a/solution.py
+++ b/solution.py
@@ -20,6 +20,7 @@
 PART = 16
 HALO = 8
 SUBS = 4
+RING_SENDS = {2: 1, 8: 7}
 
 NN = (((1,), (0,)), ((), ()))
 NT = (((1,), (1,)), ((), ()))
@@ -111,20 +112,23 @@
     def arrived(dst, recv):
         remote(dst, dst, recv, recv, partner).wait_recv()
 
+    def settle(shape_of, sem):
+        pltpu.make_async_copy(shape_of, shape_of, sem).wait()
+
     loads = [
-        pltpu.make_async_copy(w, weights.at[:, pl.ds(i * HD, HD)], load_sem.at[i])
+        pltpu.make_async_copy(w, weights.at[:, pl.ds(i * HD, HD)], load_sem.at[0])
         for i, w in enumerate((wq, wk, wv))
     ]
-    own_wo = pltpu.make_async_copy(wo, outw.at[h], load_sem.at[3])
+    own_wo = pltpu.make_async_copy(wo, outw.at[h], load_sem.at[1])
     small = [
-        pltpu.make_async_copy(src, dst, load_sem.at[6 + i])
+        pltpu.make_async_copy(src, dst, load_sem.at[3 + i])
         for i, (src, dst) in enumerate(
             ((wb_in, wb), (bias_in, bias), (conv_in, conv), (gain_in, gain))
         )
     ]
     own_tok = [
         pltpu.make_async_copy(
-            tok.at[pl.ds(i * PART, PART)], gathered.at[y, c, i], load_sem.at[10 + i]
+            tok.at[pl.ds(i * PART, PART)], gathered.at[y, c, i], load_sem.at[2]
         )
         for i in range(4)
     ]
@@ -159,32 +163,25 @@
         10 + (x_chips - 1) + jnp.where(s > 0, 1, 0) + jnp.where(sends_halo, 8, 0),
     )
 
-    sent = []
-
-    def tok_copy(src, yy, cc, half, device):
-        copy = remote(
-            src, gathered.at[yy, cc, half],
-            tok_send.at[len(sent)], tok_recv.at[yy, cc, half], device,
-        )
-        copy.start()
-        sent.append(copy)
+    def tok_copy(src, yy, cc, part, device, kind):
+        recv = tok_recv.at[yy, 4] if device is partner else tok_recv.at[yy, part]
+        remote(src, gathered.at[yy, cc, part], tok_send.at[kind], recv, device).start()
 
     def relay(yy, half, device):
-        tok_copy(gathered.at[yy, c, half], yy, c, half, device)
+        tok_copy(gathered.at[yy, c, half], yy, c, half, device, 1)
 
     to_up, to_down = (s, head_of(up, c)), (s, head_of(down, c))
-    for copy in own_tok:
-        copy.wait()
+    settle(gathered.at[y, c], load_sem.at[2])
     own = [gathered.at[y, c, i] for i in range(4)]
     for first, second in ((0, 2), (1, 3), (2, 0), (3, 1)):
-        tok_copy(own[first], y, c, first, to_up)
-        tok_copy(own[second], y, c, second, to_down)
+        tok_copy(own[first], y, c, first, to_up, 0)
+        tok_copy(own[second], y, c, second, to_down, 0)
     for i in range(4):
-        tok_copy(own[i], y, c, i, partner)
+        tok_copy(own[i], y, c, i, partner, 0)
 
     def halo_copy(peer):
         return remote(
-            tok.at[pl.ds(ROWS - HALO, HALO)], halo, halo_send.at[peer], halo_recv, (s + 1, peer)
+            tok.at[pl.ds(ROWS - HALO, HALO)], halo, halo_send, halo_recv, (s + 1, peer)
         )
 
     @pl.when(sends_halo)
@@ -200,8 +197,7 @@
         copy.wait()
     rate_rows = jnp.broadcast_to(wb[...].astype(F32), (HD, D))
     weights[:, pl.ds(3 * HD, HD)] = jnp.transpose(rate_rows).astype(BF16)
-    for copy in loads:
-        copy.wait()
+    settle(weights.at[:, pl.ds(0, 3 * HD)], load_sem.at[0])
 
     def project(yy):
         block = gathered[yy].reshape(CHUNK, D)
@@ -210,23 +206,25 @@
         padded[pl.ds(start + HALO, CHUNK), :] = result[:, : 3 * HD].astype(BF16).astype(F32)
         logits[pl.ds(start, CHUNK), :] = result[:, 3 * HD :]
 
-    def tok_arrived(yy, cc, half):
-        arrived(gathered.at[yy, cc, half], tok_recv.at[yy, cc, half])
+    def tok_arrived(yy, part):
+        arrived(gathered.at[yy, c, part], tok_recv.at[yy, part])
+
+    def tok_other_arrived(yy):
+        arrived(gathered.at[yy, other], tok_recv.at[yy, 4])
 
     def near_arrived(up_part, down_part, onward):
-        tok_arrived(down, c, up_part)
+        tok_arrived(down, up_part)
         if onward:
             relay(down, up_part, to_up)
         relay(down, up_part, partner)
-        tok_arrived(up, c, down_part)
+        tok_arrived(up, down_part)
         if onward:
             relay(up, down_part, to_down)
         relay(up, down_part, partner)
 
     near_arrived(0, 2, True)
     near_arrived(1, 3, True)
-    for part in range(4):
-        tok_arrived(y, other, part)
+    tok_other_arrived(y)
     project(y)
     near_arrived(2, 0, False)
     near_arrived(3, 1, False)
@@ -237,34 +235,28 @@
     edge = dot(halo[...], weights[...])[:, : 3 * HD].astype(BF16).astype(F32)
     padded[pl.ds(0, HALO), :] = edge
     for part in (0, 2, 1, 3):
-        tok_arrived(far, c, part)
+        tok_arrived(far, part)
         relay(far, part, partner)
     for yy in (down, up):
-        for part in range(4):
-            tok_arrived(yy, other, part)
+        tok_other_arrived(yy)
         project(yy)
-    for part in range(4):
-        tok_arrived(far, other, part)
+    tok_other_arrived(far)
     project(far)
 
     own_wo.wait()
-    wo_sent = []
 
     def wo_copy(src, slot, half, device):
-        copy = remote(
-            src.at[pl.ds(half * ROWS, ROWS)], outw.at[slot, pl.ds(half * ROWS, ROWS)],
-            w_send.at[len(wo_sent)], w_recv.at[slot, half], device,
-        )
-        copy.start()
-        wo_sent.append(copy)
+        rows = pl.ds(half * ROWS, ROWS)
+        recv = w_recv.at[slot // 2, 2 if device is partner else half]
+        remote(src.at[rows], outw.at[slot, rows], w_send, recv, device).start()
 
     def wo_relay(yy, half, device):
         slot = head_of(yy, c)
         wo_copy(outw.at[slot], slot, half, device)
 
-    def wo_arrived(yy, cc, half):
-        slot = head_of(yy, cc)
-        arrived(outw.at[slot, pl.ds(half * ROWS, ROWS)], w_recv.at[slot, half])
+    def wo_arrived(yy, half):
+        slot = head_of(yy, c)
+        arrived(outw.at[slot, pl.ds(half * ROWS, ROWS)], w_recv.at[yy, half])
 
     wo_copy(outw.at[h], h, 0, to_up)
     wo_copy(outw.at[h], h, 1, to_down)
@@ -275,17 +267,17 @@
 
     def wo_relay_near():
         for yy, first, onward in ((down, 0, to_up), (up, 1, to_down)):
-            wo_arrived(yy, c, first)
+            wo_arrived(yy, first)
             wo_relay(yy, first, onward)
         for yy in (down, up):
             for half in range(2):
                 if (yy is down) == (half == 1):
-                    wo_arrived(yy, c, half)
+                    wo_arrived(yy, half)
                 wo_relay(yy, half, partner)
 
     def wo_relay_far():
         for half in range(2):
-            wo_arrived(far, c, half)
+            wo_arrived(far, half)
             wo_relay(far, half, partner)
 
     row = lax.broadcasted_iota(jnp.int32, (CHUNK, CHUNK), 0)
@@ -363,52 +355,55 @@
     pairs = z_chips // 2
     j = z // 2
     ring[j] = own_f[...].astype(BF16).reshape(SUBS, 2 * HD // SUBS, HD)
-    ring_sent = []
     two_up = (x * z_chips + (z + 2) % z_chips, h)
     two_down = (x * z_chips + (z + z_chips - 2) % z_chips, h)
 
     def ring_copy(slot, q, device):
-        copy = remote(
-            ring.at[slot, q], ring.at[slot, q],
-            ring_send.at[len(ring_sent)], ring_recv.at[slot, q], device,
-        )
-        copy.start()
-        ring_sent.append(copy)
-
-    reach_left, reach_right = pairs // 2, (pairs - 1) // 2
+        remote(
+            ring.at[slot, q], ring.at[slot, q], ring_send, ring_recv.at[slot, q], device
+        ).start()
+
+    reach = pairs // 2
+
+    def ring_pass(slot, q, step):
+        if step < reach or (step == reach and q < SUBS // 2):
+            ring_copy(slot, q, two_up)
+
+    def ring_pass_down(slot, q, step):
+        if step < reach or (step == reach and q >= SUBS // 2):
+            ring_copy(slot, q, two_down)
+
     for q in range(SUBS):
-        ring_copy(j, q, two_up)
-        if reach_right > 0:
-            ring_copy(j, q, two_down)
+        ring_pass(j, q, 1)
+        ring_pass_down(j, q, 1)
 
     def compose(k):
         slot = (j + pairs - k) % pairs
         side = jnp.where(k > j, 1, 0)
         left[side] = prepend(ring[slot].reshape(2 * HD, HD), left[side])
-        if k <= reach_right:
+        if k < reach:
             slot_r = (j + k) % pairs
             side_r = jnp.where(j + k >= pairs, 1, 0)
             right[side_r] = append(right[side_r], ring[slot_r].reshape(2 * HD, HD))
 
-    for k in range(1, reach_left + 1):
+    for k in range(1, reach + 1):
         slot = (j + pairs - k) % pairs
         slot_r = (j + k) % pairs
         for q in range(SUBS):
-            arrived(ring.at[slot, q], ring_recv.at[slot, q])
-            if k < reach_left:
-                ring_copy(slot, q, two_up)
-            if k <= reach_right:
+            if k < reach or q < SUBS // 2:
+                arrived(ring.at[slot, q], ring_recv.at[slot, q])
+                ring_pass(slot, q, k + 1)
+            if k < reach or q >= SUBS // 2:
                 arrived(ring.at[slot_r, q], ring_recv.at[slot_r, q])
-                if k < reach_right:
-                    ring_copy(slot_r, q, two_down)
+                ring_pass_down(slot_r, q, k + 1)
         if k == 1:
             wo_relay_near()
-        if k == max(1, reach_left - 1):
+        if k == max(1, reach - 1):
             wo_relay_far()
             for done in range(1, k + 1):
                 compose(done)
-    if reach_left > 1:
-        compose(reach_left)
+    if reach > 1:
+        compose(reach)
     before = after(right[1], left[0])
     line = after(before, after(own_f[...], after(right[0], left[1])))
     prefix[...] = before
@@ -417,27 +412,44 @@
     def _():
         prefix[...] = append(before, duo[0])
 
-    lines[x] = line.astype(BF16)
-
-    def line_copy(step):
+    lines[x] = line.astype(BF16).reshape(2, HD, HD)
+    moves = [
+        (0, 1, 0, 1), (0, 3, 0, 1), (0, 2, 0, 1), (1, 3, 1, 0), (1, 2, 1, 0),
+        (1, 2, 1, 1), (1, 0, 1, 1), (2, 3, 2, 0), (2, 3, 2, 1), (0, 3, 1, 1),
+    ]
+
+    def line_copy(i):
+        _, to, slot, part = moves[i]
         return remote(
-            lines.at[x], lines.at[x], line_send.at[step - 1], line_recv.at[x],
-            ((x + step) * z_chips + z, h),
+            lines.at[slot, part], lines.at[slot, part], line_send,
+            line_recv.at[slot, part], (to * z_chips + z, h),
         )
 
-    for step in range(1, x_chips):
-
-        @pl.when(x + step < x_chips)
-        def _():
-            line_copy(step).start()
+    def line_arrived(slot, part):
+        arrived(lines.at[slot, part], line_recv.at[slot, part])
+
+    if x_chips == 4:
+        for i, move in enumerate(moves):
+
+            @pl.when(x == move[0])
+            def _():
+                if i == len(moves) - 1:
+                    line_arrived(1, 1)
+                line_copy(i).start()
 
     entering[...] = jnp.zeros_like(entering)
     for k in range(x_chips - 1):
 
         @pl.when(k < x)
         def _():
-            arrived(lines.at[k], line_recv.at[k])
-            entering[...] = mm_state(entering[...], lines[k])
+            line_arrived(k, 1)
+            if k == 0:
+                entering[...] = lines[0, 1].astype(F32)
+            else:
+                line_arrived(k, 0)
+                high, low = split(entering[...])
+                step = lines[k, 0]
+                entering[...] = dot(high, step) + dot(low, step) + lines[k, 1].astype(F32)
 
     state = mm3(entering[...], prefix[pl.ds(0, HD)]) + prefix[pl.ds(HD, HD)]
 
@@ -447,43 +459,39 @@
     normed = (outputs * scale * gain[...]).astype(BF16)
     for peer in range(8):
         give[peer] = normed[peer * ROWS : (peer + 1) * ROWS]
-    handed = []
-    for step in range(1, 8):
-        peer = (h + step) % 8
-        copy = remote(
-            give.at[peer], got.at[h], give_send.at[step - 1], got_recv.at[h], (s, peer)
-        )
-        copy.start()
-        handed.append(copy)
+    order = [head_of(yy, cc) for yy, cc in (
+        (far, c), (far, other), (up, c), (down, c), (up, other), (down, other), (y, other)
+    )]
+    for peer in order:
+        remote(give.at[peer], got.at[h], give_send, got_recv, (s, peer)).start()
     got[h] = give[h]
     for yy in (y, up, down, far):
-        for half in range(2):
-            wo_arrived(yy, other, half)
-    for step in range(1, 8):
-        peer = (h + step) % 8
-        arrived(got.at[peer], got_recv.at[peer])
+        arrived(outw.at[head_of(yy, other)], w_recv.at[yy, 2])
+    settle(got.at[pl.ds(0, 7)], got_recv)
     mixed = jnp.zeros((ROWS, D), F32)
     for g in range(8):
         mixed = mixed + dot(got[g], outw[g]).astype(BF16).astype(F32)
     out[...] = mixed.astype(BF16)
 
-    for copy in (*sent, *wo_sent, duo_copy, *ring_sent, *handed):
-        copy.wait_send()
-    for step in range(1, x_chips):
-
-        @pl.when(x + step < x_chips)
+    settle(gathered.at[pl.ds(0, 3), 0], tok_send.at[0])
+    settle(gathered.at[:, 0], tok_send.at[1])
+    settle(outw.at[pl.ds(0, 7)], w_send)
+    settle(ring.at[pl.ds(0, RING_SENDS[pairs])], ring_send)
+    settle(give.at[pl.ds(0, 7)], give_send)
+    duo_copy.wait_send()
+    if x_chips == 4:
+
+        @pl.when(x < 2)
         def _():
-            line_copy(step).wait_send()
+            settle(lines.at[pl.ds(0, 2)], line_send)
+
+        @pl.when(x == 2)
+        def _():
+            settle(lines.at[0], line_send)
 
     @pl.when(sends_halo)
     def _():
-        for peer in range(8):
-            halo_copy(peer).wait_send()
-
-
-def mm_state(state, raw):
-    high, low = split(state)
-    return dot(high, raw[:HD]) + dot(low, raw[:HD]) + raw[HD:].astype(F32)
+        settle(gathered.at[0, 0], halo_send)
 
 
 def local(x_chips, z_chips, tokens, w_query, w_key, w_value, w_beta, beta_bias, conv_weight, norm_gain, w_out):
@@ -509,7 +517,7 @@
             pltpu.VMEM((SHARD, HD), BF16),
             pltpu.VMEM((SHARD, HD), F32),
             pltpu.VMEM((z_chips // 2, SUBS, 2 * HD // SUBS, HD), BF16),
-            pltpu.VMEM((x_chips, 2 * HD, HD), BF16),
+            pltpu.VMEM((x_chips, 2, HD, HD), BF16),
             pltpu.VMEM((2, 2 * HD, HD), F32),
             pltpu.VMEM((2, 2 * HD, HD), F32),
             pltpu.VMEM((2 * HD, HD), F32),
@@ -518,30 +526,34 @@
             pltpu.VMEM((HD, HD), F32),
             pltpu.VMEM((8, ROWS, HD), BF16),
             pltpu.VMEM((8, ROWS, HD), BF16),
-            dma((14,)),
-            dma((28,)),
-            dma((Y_CHIPS, 2, 4)),
-            dma((8,)),
-            dma,
-            dma((14,)),
-            dma((8, 2)),
-            dma,
+            dma((7,)),
             dma((2,)),
-            dma((z_chips // 2 * SUBS,)),
+            dma((Y_CHIPS, 5)),
+            dma,
+            dma,
+            dma,
+            dma((Y_CHIPS, 3)),
+            dma,
+            dma((2,)),
+            dma,
             dma((z_chips // 2, SUBS)),
-            dma((x_chips,)),
-            dma((x_chips,)),
-            dma((7,)),
-            dma((8,)),
+            dma,
+            dma((x_chips, 2)),
+            dma,
+            dma,
         ],
         compiler_params=pltpu.CompilerParams(
-            collective_id=0, has_side_effects=True, vmem_limit_bytes=67043328
+            collective_id=0, has_side_effects=True, vmem_limit_bytes=48 * 1024 * 1024
         ),
     )(
-        tokens, w_query, w_key, w_value,
-        w_beta.reshape(1, D), beta_bias, conv_weight,
-        norm_gain.reshape(1, HD), w_out,
+        keep(tokens), keep(w_query), keep(w_key), keep(w_value),
+        keep(w_beta.reshape(1, D)), beta_bias, keep(conv_weight),
+        keep(norm_gain.reshape(1, HD)), keep(w_out),
     )
+
+
+def keep(a):
+    return pltpu.with_memory_space_constraint(a, pltpu.HBM)
 
 
 def solution(mesh):

time: 63.4 us -> 60.8 us (0.959)
  the two profiles are of different devices: /device:TPU:37 before, /device:TPU:39 now
where the time goes in v3:
time: 60.8 us; the launch traced here: 60.6 us
  Pallas kernels  59.3 us (98%)
  local copies, waits for them, and re-layouts  0.66 us (1%)
  between operations  0.66 us (1%)
    pallas_call x1, Pallas kernels, local(): pl.pallas_call(functools.partial(layer, x_chips, z_chips), out_shape=jax....  59.3 us

profile of v3, /device:TPU:39, one launch (start us, length us, event | category | flops | bytes accessed | tf_op | source)
XLA Modules:
  0.0 60.6 jit_solution(5141778337679345384)
XLA Ops:
  0.7 59.3 %shard_map.91 = bf16[64,1024]{1,0:T(8,128)(2,1)S(1)} custom-call(bf16[64,1024]{1,0:T(8,128)(2,1)} %tok.1, bf16[1024,128]{1,0:T(8,128)(2,1)} %wq.1, bf16[1024,128]{1,0:T(8,128)(2,1)} %wk.1, bf16[1024,128]{1,0:T(8,128)(2,1)} %wv.1, bf16[1,1024]{1,0:T(2,128)(2,1)} %bitcast.2, f32[1]{0:T(128)S(6)} %copy.11.bias_in, f32[3,4,128]{2,1,0:T(4,128)} %conv_in.1, ...), custom_call_target="tpu_custom_call" | custom-call | tf_op jit(solution)/shard_map/pallas_call | solution.py:501
  60.0 0.7 %copy.12 = bf16[64,1024]{1,0:T(8,128)(2,1)} copy(bf16[64,1024]{1,0:T(8,128)(2,1)S(1)} %shard_map.91) | data formatting | bytes 262144

commit v4 on v3

--- a/solution.py
+++ b/solution.py
@@ -20,6 +20,7 @@
 PART = 16
 HALO = 8
 SUBS = 4
+HALF_SUBS = SUBS // 2
 RING_SENDS = {2: 1, 8: 7}
 
 NN = (((1,), (0,)), ((), ()))
@@ -86,7 +87,7 @@
     out,
     wb, bias, conv, gain,
     gathered, halo, weights, outw, padded, logits,
-    q_eff, o_loc, ring, lines, left, right, own_f, prefix, duo, entering,
+    q_eff, o_loc, ring, lines, left, right, own_f, prefix, duo, mate, next_state, state, entering,
     give, got,
     load_sem, tok_send, tok_recv, halo_send, halo_recv, w_send, w_recv,
     duo_send, duo_recv, ring_send, ring_recv, line_send, line_recv, give_send, got_recv,
@@ -142,7 +143,10 @@
 
     for step in range(1, 8):
         greet((s, (h + step) % 8))
-    for hops in (z + 1 - 2 * (z % 2), (z + 2) % z_chips, (z + z_chips - 2) % z_chips):
+    near = [z + 1 - 2 * (z % 2)]
+    for offset in (2, 4) if z_chips == 16 else (2,):
+        near += [(z + offset) % z_chips, (z + z_chips - offset) % z_chips]
+    for hops in near:
         greet((x * z_chips + hops, h))
     for step in range(1, x_chips):
         greet((((x + step) % x_chips) * z_chips + z, h))
@@ -160,7 +164,7 @@
 
     pl.semaphore_wait(
         barrier,
-        10 + (x_chips - 1) + jnp.where(s > 0, 1, 0) + jnp.where(sends_halo, 8, 0),
+        7 + len(near) + (x_chips - 1) + jnp.where(s > 0, 1, 0) + jnp.where(sends_halo, 8, 0),
     )
 
     def tok_copy(src, yy, cc, part, device, kind):
@@ -331,129 +335,142 @@
                 o_loc[pl.ds(n * CHUNK, CHUNK), :] = turned[:, HD:] + reach[:, HD:]
 
 
-    halves = z % 2
-    z_other = z + 1 - 2 * halves
-    duo[halves] = before.astype(BF16)
-    duo_copy = remote(
-        duo.at[halves], duo.at[halves], duo_send, duo_recv.at[halves], (x * z_chips + z_other, h)
-    )
-    duo_copy.start()
-    finish_outputs()
-    for i in range(2):
-        left[i] = lead
-        right[i] = lead
-    arrived(duo.at[1 - halves], duo_recv.at[1 - halves])
-
-    @pl.when(halves == 0)
-    def _():
-        own_f[...] = append(before, duo[1])
-
-    @pl.when(halves == 1)
-    def _():
-        own_f[...] = prepend(duo[0], before)
-
+    odd = z % 2
     pairs = z_chips // 2
     j = z // 2
-    ring[j] = own_f[...].astype(BF16).reshape(SUBS, 2 * HD // SUBS, HD)
-    two_up = (x * z_chips + (z + 2) % z_chips, h)
-    two_down = (x * z_chips + (z + z_chips - 2) % z_chips, h)
-
-    def ring_copy(slot, q, device):
+
+    def at_z(offset):
+        return (x * z_chips + (z + z_chips + offset) % z_chips, h)
+
+    duo[...] = before.astype(BF16)
+    to_even = remote(duo, mate, duo_send.at[0], duo_recv.at[0], at_z(-1))
+    to_odd = remote(next_state, next_state, duo_send.at[1], duo_recv.at[1], at_z(1))
+
+    @pl.when(odd == 1)
+    def _():
+        to_even.start()
+
+    finish_outputs()
+
+    def ring_copy(slot, q, offset, sem):
         remote(
-            ring.at[slot, q], ring.at[slot, q], ring_send, ring_recv.at[slot, q], device
+            ring.at[slot, q], ring.at[slot, q], ring_send, ring_recv.at[slot, sem],
+            at_z(2 * offset),
         ).start()
-
-    reach = pairs // 2
-
-    def ring_pass(slot, q, step):
-        if step < reach or (step == reach and q < SUBS // 2):
-            ring_copy(slot, q, two_up)
-
-    def ring_pass_down(slot, q, step):
-        if step < reach or (step == reach and q >= SUBS // 2):
-            ring_copy(slot, q, two_down)
-
-    for q in range(SUBS):
-        ring_pass(j, q, 1)
-        ring_pass_down(j, q, 1)
 
     def compose(k):
         slot = (j + pairs - k) % pairs
         side = jnp.where(k > j, 1, 0)
         left[side] = prepend(ring[slot].reshape(2 * HD, HD), left[side])
-        if k < reach:
+        if 2 * k < pairs:
             slot_r = (j + k) % pairs
             side_r = jnp.where(j + k >= pairs, 1, 0)
             right[side_r] = append(right[side_r], ring[slot_r].reshape(2 * HD, HD))
 
-    for k in range(1, reach + 1):
-        slot = (j + pairs - k) % pairs
-        slot_r = (j + k) % pairs
-        for q in range(SUBS):
-            if k < reach or q < SUBS // 2:
-                arrived(ring.at[slot, q], ring_recv.at[slot, q])
-                ring_pass(slot, q, k + 1)
-            if k < reach or q >= SUBS // 2:
-                arrived(ring.at[slot_r, q], ring_recv.at[slot_r, q])
-                ring_pass_down(slot_r, q, k + 1)
-        if k == 1:
+    def ring_arrived(k):
+        if 2 * k < pairs:
+            for slot in ((j + pairs - k) % pairs, (j + k) % pairs):
+                arrived(ring.at[slot], ring_recv.at[slot, 0])
+        else:
+            slot = (j + k) % pairs
+            for side in range(2):
+                arrived(ring.at[slot, pl.ds(side * HALF_SUBS, HALF_SUBS)], ring_recv.at[slot, side])
+
+    def scan_pairs():
+        for i in range(2):
+            left[i] = lead
+            right[i] = lead
+        arrived(mate, duo_recv.at[0])
+        own_f[...] = append(before, mate[...])
+        ring[j] = own_f[...].astype(BF16).reshape(SUBS, 2 * HD // SUBS, HD)
+        if pairs == 8:
+            for q in range(SUBS):
+                ring_copy(j, q, 2, q)
+                ring_copy(j, q, -2, q)
+            for q in range(SUBS):
+                ring_copy(j, q, 1, 0)
+                ring_copy(j, q, -1, 0)
+            back, ahead = (j + pairs - 2) % pairs, (j + 2) % pairs
+            for q in range(SUBS):
+                arrived(ring.at[back, q], ring_recv.at[back, q])
+                if q < HALF_SUBS:
+                    ring_copy(back, q, 2, 0)
+                ring_copy(back, q, 1, 0)
+                arrived(ring.at[ahead, q], ring_recv.at[ahead, q])
+                if q >= HALF_SUBS:
+                    ring_copy(ahead, q, -2, 1)
+                ring_copy(ahead, q, -1, 0)
             wo_relay_near()
-        if k == max(1, reach - 1):
+            ring_arrived(1)
+            compose(1)
+            compose(2)
             wo_relay_far()
-            for done in range(1, k + 1):
-                compose(done)
-    if reach > 1:
-        compose(reach)
-    before = after(right[1], left[0])
-    line = after(before, after(own_f[...], after(right[0], left[1])))
-    prefix[...] = before
-
-    @pl.when(halves == 1)
-    def _():
-        prefix[...] = append(before, duo[0])
-
-    lines[x] = line.astype(BF16).reshape(2, HD, HD)
-    moves = [
-        (0, 1, 0, 1), (0, 3, 0, 1), (0, 2, 0, 1), (1, 3, 1, 0), (1, 2, 1, 0),
-        (1, 2, 1, 1), (1, 0, 1, 1), (2, 3, 2, 0), (2, 3, 2, 1), (0, 3, 1, 1),
-    ]
-
-    def line_copy(i):
-        _, to, slot, part = moves[i]
-        return remote(
-            lines.at[slot, part], lines.at[slot, part], line_send,
-            line_recv.at[slot, part], (to * z_chips + z, h),
-        )
-
-    def line_arrived(slot, part):
-        arrived(lines.at[slot, part], line_recv.at[slot, part])
-
-    if x_chips == 4:
-        for i, move in enumerate(moves):
-
-            @pl.when(x == move[0])
+            ring_arrived(3)
+            compose(3)
+        else:
+            for q in range(SUBS):
+                ring_copy(j, q, 1 if q < HALF_SUBS else -1, q // HALF_SUBS)
+            wo_relay_near()
+            wo_relay_far()
+        ring_arrived(pairs // 2)
+        compose(pairs // 2)
+        prefix[...] = after(right[1], left[0])
+        line = after(prefix[...], after(own_f[...], after(right[0], left[1])))
+
+        lines[x] = line.astype(BF16).reshape(2, HD, HD)
+        moves = [
+            (0, 2, 1), (0, 1, 1), (0, 3, 1), (1, 3, 0), (1, 3, 1),
+            (1, 2, 0), (1, 2, 1), (2, 3, 0), (2, 3, 1),
+        ]
+
+        def line_copy(i):
+            slot, to, part = moves[i]
+            return remote(
+                lines.at[slot, part], lines.at[slot, part], line_send,
+                line_recv.at[slot, part], (to * z_chips + z, h),
+            )
+
+        def line_arrived(slot, part):
+            arrived(lines.at[slot, part], line_recv.at[slot, part])
+
+        if x_chips == 4:
+            for i, move in enumerate(moves):
+
+                @pl.when(x == move[0])
+                def _():
+                    line_copy(i).start()
+
+        entering[...] = jnp.zeros_like(entering)
+        for k in range(x_chips - 1):
+
+            @pl.when(k < x)
             def _():
-                if i == len(moves) - 1:
-                    line_arrived(1, 1)
-                line_copy(i).start()
-
-    entering[...] = jnp.zeros_like(entering)
-    for k in range(x_chips - 1):
-
-        @pl.when(k < x)
-        def _():
-            line_arrived(k, 1)
-            if k == 0:
-                entering[...] = lines[0, 1].astype(F32)
-            else:
-                line_arrived(k, 0)
-                high, low = split(entering[...])
-                step = lines[k, 0]
-                entering[...] = dot(high, step) + dot(low, step) + lines[k, 1].astype(F32)
-
-    state = mm3(entering[...], prefix[pl.ds(0, HD)]) + prefix[pl.ds(HD, HD)]
-
-    high, low = split(state)
+                line_arrived(k, 1)
+                if k == 0:
+                    entering[...] = lines[0, 1].astype(F32)
+                else:
+                    line_arrived(k, 0)
+                    high, low = split(entering[...])
+                    step = lines[k, 0]
+                    entering[...] = dot(high, step) + dot(low, step) + lines[k, 1].astype(F32)
+
+        own_in = mm3(entering[...], prefix[pl.ds(0, HD)]) + prefix[pl.ds(HD, HD)]
+        next_state[...] = (mm3(own_in, before[:HD]) + before[HD:]).astype(BF16)
+        to_odd.start()
+        state[...] = own_in
+
+    @pl.when(odd == 0)
+    def _():
+        scan_pairs()
+
+    @pl.when(odd == 1)
+    def _():
+        wo_relay_near()
+        wo_relay_far()
+        arrived(next_state, duo_recv.at[1])
+        state[...] = next_state[...].astype(F32)
+
+    high, low = split(state[...])
     outputs = dot(q_eff[...], high, NT) + dot(q_eff[...], low, NT) + o_loc[...]
     scale = lax.rsqrt(jnp.mean(outputs * outputs, -1, keepdims=True) + 1e-05)
     normed = (outputs * scale * gain[...]).astype(BF16)
@@ -476,18 +493,23 @@
     settle(gathered.at[pl.ds(0, 3), 0], tok_send.at[0])
     settle(gathered.at[:, 0], tok_send.at[1])
     settle(outw.at[pl.ds(0, 7)], w_send)
-    settle(ring.at[pl.ds(0, RING_SENDS[pairs])], ring_send)
     settle(give.at[pl.ds(0, 7)], give_send)
-    duo_copy.wait_send()
+
+    @pl.when(odd == 1)
+    def _():
+        to_even.wait_send()
+
+    @pl.when(odd == 0)
+    def _():
+        to_odd.wait_send()
+        settle(ring.at[pl.ds(0, RING_SENDS[pairs])], ring_send)
+
     if x_chips == 4:
-
-        @pl.when(x < 2)
-        def _():
-            settle(lines.at[pl.ds(0, 2)], line_send)
-
-        @pl.when(x == 2)
-        def _():
-            settle(lines.at[0], line_send)
+        for line_x, count in enumerate((3, 4, 2)):
+
+            @pl.when((odd == 0) & (x == line_x))
+            def _():
+                settle(lines.at[pl.ds(0, count), 0], line_send)
 
     @pl.when(sends_halo)
     def _():
@@ -522,7 +544,10 @@
             pltpu.VMEM((2, 2 * HD, HD), F32),
             pltpu.VMEM((2 * HD, HD), F32),
             pltpu.VMEM((2 * HD, HD), F32),
-            pltpu.VMEM((2, 2 * HD, HD), BF16),
+            pltpu.VMEM((2 * HD, HD), BF16),
+            pltpu.VMEM((2 * HD, HD), BF16),
+            pltpu.VMEM((HD, HD), BF16),
+            pltpu.VMEM((HD, HD), F32),
             pltpu.VMEM((HD, HD), F32),
             pltpu.VMEM((8, ROWS, HD), BF16),
             pltpu.VMEM((8, ROWS, HD), BF16),
@@ -533,7 +558,7 @@
             dma,
             dma,
             dma((Y_CHIPS, 3)),
-            dma,
+            dma((2,)),
             dma((2,)),
             dma,
             dma((z_chips // 2, SUBS)),

time: 60.8 us -> 56.4 us (0.928)
  Pallas kernels: 59.3 us -> 55 us
    pallas_call x1, Pallas kernels: 59.3 us -> 55 us  [local(): pl.pallas_call(functools.partial(layer, x_chips, z_chips), out_shape=jax....]
where the time goes in v4:
time: 56.4 us; the launch traced here: 56.3 us
  Pallas kernels  55 us (98%)
  local copies, waits for them, and re-layouts  0.66 us (1%)
  between operations  0.66 us (1%)
    pallas_call x1, Pallas kernels, local(): pl.pallas_call(functools.partial(layer, x_chips, z_chips), out_shape=jax....  55 us

profile of v4, /device:TPU:39, one launch (start us, length us, event | category | flops | bytes accessed | tf_op | source)
XLA Modules:
  0.0 56.3 jit_solution(17296945576397801966)
XLA Ops:
  0.7 55.0 %shard_map.91 = bf16[64,1024]{1,0:T(8,128)(2,1)S(1)} custom-call(bf16[64,1024]{1,0:T(8,128)(2,1)} %tok.1, bf16[1024,128]{1,0:T(8,128)(2,1)} %wq.1, bf16[1024,128]{1,0:T(8,128)(2,1)} %wk.1, bf16[1024,128]{1,0:T(8,128)(2,1)} %wv.1, bf16[1,1024]{1,0:T(2,128)(2,1)} %bitcast.2, f32[1]{0:T(128)S(6)} %copy.11.bias_in, f32[3,4,128]{2,1,0:T(4,128)} %conv_in.1, ...), custom_call_target="tpu_custom_call" | custom-call | tf_op jit(solution)/shard_map/pallas_call | solution.py:523
  55.6 0.7 %copy.12 = bf16[64,1024]{1,0:T(8,128)(2,1)} copy(bf16[64,1024]{1,0:T(8,128)(2,1)S(1)} %shard_map.91) | data formatting | bytes 262144

commit v5 on v4

--- a/solution.py
+++ b/solution.py
@@ -38,9 +38,12 @@
 
 
 def mm3(a, b):
-    ah, al = split(a)
     bh, bl = split(b)
-    return dot(ah, bh) + (dot(ah, bl) + dot(al, bh))
+    wide = b.shape[1]
+    pair = jnp.concatenate([bh, bl], 1)
+    alone = jnp.concatenate([bh, jnp.zeros_like(bh)], 1)
+    both = dot(jnp.concatenate(split(a), 1), jnp.concatenate([pair, alone], 0))
+    return both[:, :wide] + both[:, wide:]
 
 
 def after(earlier, later):
@@ -52,14 +55,16 @@
 
 
 def prepend(raw, acc):
-    high, low = split(acc[:HD])
-    return dot(raw, high) + dot(raw, low) + pad_top(acc[HD:])
+    both = dot(raw, jnp.concatenate(split(acc[:HD]), 1))
+    return both[:, :HD] + both[:, HD:] + pad_top(acc[HD:])
+
+
+def twice(a, b):
+    return dot(jnp.concatenate(split(a), 1), jnp.concatenate([b, b], 0))
 
 
 def append(acc, raw):
-    high, low = split(acc)
-    step = raw[:HD]
-    return dot(high, step) + dot(low, step) + pad_top(raw[HD:].astype(F32))
+    return twice(acc, raw[:HD]) + pad_top(raw[HD:].astype(F32))
 
 
 def invert(lowers):
@@ -316,7 +321,7 @@
         query, key = parts[n]
         solved = mm3(inverses[n], rights[n])
         high, low = split(solved)
-        moved = dot(high, key, TN) + dot(low, key, TN)
+        moved = dot(jnp.concatenate([high, low], 0), jnp.concatenate([key, key], 0), TN)
         step = jnp.concatenate([eye - moved[:HD], moved[HD:]], 0)
         entry.append(before)
         reached.append(high)
@@ -450,9 +455,7 @@
                     entering[...] = lines[0, 1].astype(F32)
                 else:
                     line_arrived(k, 0)
-                    high, low = split(entering[...])
-                    step = lines[k, 0]
-                    entering[...] = dot(high, step) + dot(low, step) + lines[k, 1].astype(F32)
+                    entering[...] = twice(entering[...], lines[k, 0]) + lines[k, 1].astype(F32)
 
         own_in = mm3(entering[...], prefix[pl.ds(0, HD)]) + prefix[pl.ds(HD, HD)]
         next_state[...] = (mm3(own_in, before[:HD]) + before[HD:]).astype(BF16)
@@ -470,30 +473,33 @@
         arrived(next_state, duo_recv.at[1])
         state[...] = next_state[...].astype(F32)
 
-    high, low = split(state[...])
-    outputs = dot(q_eff[...], high, NT) + dot(q_eff[...], low, NT) + o_loc[...]
-    scale = lax.rsqrt(jnp.mean(outputs * outputs, -1, keepdims=True) + 1e-05)
-    normed = (outputs * scale * gain[...]).astype(BF16)
-    for peer in range(8):
-        give[peer] = normed[peer * ROWS : (peer + 1) * ROWS]
-    order = [head_of(yy, cc) for yy, cc in (
-        (far, c), (far, other), (up, c), (down, c), (up, other), (down, other), (y, other)
-    )]
-    for peer in order:
-        remote(give.at[peer], got.at[h], give_send, got_recv, (s, peer)).start()
-    got[h] = give[h]
+    terms = jnp.concatenate(split(state[...]), 0)
+    for yy in (far, up, down, y):
+        rows = pl.ds(pl.multiple_of(yy * CHUNK, CHUNK), CHUNK)
+        both = dot(q_eff[rows, :], terms, NT)
+        outputs = both[:, :HD] + both[:, HD:] + o_loc[rows, :]
+        scale = lax.rsqrt(jnp.mean(outputs * outputs, -1, keepdims=True) + 1e-05)
+        give[yy] = (outputs * scale * gain[...]).astype(BF16).reshape(2, ROWS, HD)
+        for cc in (c, other) if yy is not y else (other,):
+            remote(
+                give.at[yy, cc], got.at[h], give_send, got_recv.at[h], (s, head_of(yy, cc))
+            ).start()
+    got[h] = give[y, c]
     for yy in (y, up, down, far):
         arrived(outw.at[head_of(yy, other)], w_recv.at[yy, 2])
-    settle(got.at[pl.ds(0, 7)], got_recv)
-    mixed = jnp.zeros((ROWS, D), F32)
-    for g in range(8):
-        mixed = mixed + dot(got[g], outw[g]).astype(BF16).astype(F32)
+    mixed = dot(got[h], outw[h]).astype(BF16).astype(F32)
+    for peer in (
+        head_of(y, other), head_of(up, c), head_of(down, c), head_of(up, other),
+        head_of(down, other), head_of(far, c), head_of(far, other),
+    ):
+        arrived(got.at[peer], got_recv.at[peer])
+        mixed = mixed + dot(got[peer], outw[peer]).astype(BF16).astype(F32)
     out[...] = mixed.astype(BF16)
 
     settle(gathered.at[pl.ds(0, 3), 0], tok_send.at[0])
     settle(gathered.at[:, 0], tok_send.at[1])
     settle(outw.at[pl.ds(0, 7)], w_send)
-    settle(give.at[pl.ds(0, 7)], give_send)
+    settle(got.at[pl.ds(0, 7)], give_send)
 
     @pl.when(odd == 1)
     def _():
@@ -549,7 +555,7 @@
             pltpu.VMEM((HD, HD), BF16),
             pltpu.VMEM((HD, HD), F32),
             pltpu.VMEM((HD, HD), F32),
-            pltpu.VMEM((8, ROWS, HD), BF16),
+            pltpu.VMEM((Y_CHIPS, 2, ROWS, HD), BF16),
             pltpu.VMEM((8, ROWS, HD), BF16),
             dma((7,)),
             dma((2,)),
@@ -565,7 +571,7 @@
             dma,
             dma((x_chips, 2)),
             dma,
-            dma,
+            dma((8,)),
         ],
         compiler_params=pltpu.CompilerParams(
             collective_id=0, has_side_effects=True, vmem_limit_bytes=48 * 1024 * 1024

time: 56.4 us -> 56.1 us (level)
  no operation moved by 1% of the time
where the time goes in v5:
time: 56.1 us; the launch traced here: 55.9 us
  Pallas kernels  54.6 us (97%)
  local copies, waits for them, and re-layouts  0.66 us (1%)
  between operations  0.66 us (1%)
    pallas_call x1, Pallas kernels, local(): pl.pallas_call(functools.partial(layer, x_chips, z_chips), out_shape=jax....  54.6 us

profile of v5, /device:TPU:39, one launch (start us, length us, event | category | flops | bytes accessed | tf_op | source)
XLA Modules:
  0.0 55.9 jit_solution(18119000282057552005)
XLA Ops:
  0.7 54.6 %shard_map.91 = bf16[64,1024]{1,0:T(8,128)(2,1)S(1)} custom-call(bf16[64,1024]{1,0:T(8,128)(2,1)} %tok.1, bf16[1024,128]{1,0:T(8,128)(2,1)} %wq.1, bf16[1024,128]{1,0:T(8,128)(2,1)} %wk.1, bf16[1024,128]{1,0:T(8,128)(2,1)} %wv.1, bf16[1,1024]{1,0:T(2,128)(2,1)} %bitcast.2, f32[1]{0:T(128)S(6)} %copy.11.bias_in, f32[3,4,128]{2,1,0:T(4,128)} %conv_in.1, ...), custom_call_target="tpu_custom_call" | custom-call | tf_op jit(solution)/shard_map/pallas_call | solution.py:529
  55.3 0.7 %copy.12 = bf16[64,1024]{1,0:T(8,128)(2,1)} copy(bf16[64,1024]{1,0:T(8,128)(2,1)S(1)} %shard_map.91) | data formatting | bytes 262144

commit v6 on v5

--- a/solution.py
+++ b/solution.py
@@ -148,13 +148,17 @@
 
     for step in range(1, 8):
         greet((s, (h + step) % 8))
-    near = [z + 1 - 2 * (z % 2)]
-    for offset in (2, 4) if z_chips == 16 else (2,):
-        near += [(z + offset) % z_chips, (z + z_chips - offset) % z_chips]
-    for hops in near:
-        greet((x * z_chips + hops, h))
-    for step in range(1, x_chips):
-        greet((((x + step) % x_chips) * z_chips + z, h))
+    odd = z % 2
+    greet((x * z_chips + z + 1 - 2 * odd, h))
+    offsets = (2, 4) if z_chips == 16 else (2,)
+
+    @pl.when(odd == 0)
+    def _():
+        for offset in offsets:
+            greet((x * z_chips + (z + offset) % z_chips, h))
+            greet((x * z_chips + (z + z_chips - offset) % z_chips, h))
+        for step in range(1, x_chips):
+            greet((((x + step) % x_chips) * z_chips + z, h))
 
     @pl.when(s > 0)
     def _():
@@ -169,7 +173,7 @@
 
     pl.semaphore_wait(
         barrier,
-        7 + len(near) + (x_chips - 1) + jnp.where(s > 0, 1, 0) + jnp.where(sends_halo, 8, 0),
+        8 + jnp.where(odd == 0, 2 * len(offsets) + x_chips - 1, 0) + jnp.where(s > 0, 1, 0) + jnp.where(sends_halo, 8, 0),
     )
 
     def tok_copy(src, yy, cc, part, device, kind):
@@ -340,7 +344,6 @@
                 o_loc[pl.ds(n * CHUNK, CHUNK), :] = turned[:, HD:] + reach[:, HD:]
 
 
-    odd = z % 2
     pairs = z_chips // 2
     j = z // 2
 
@@ -474,16 +477,16 @@
         state[...] = next_state[...].astype(F32)
 
     terms = jnp.concatenate(split(state[...]), 0)
-    for yy in (far, up, down, y):
-        rows = pl.ds(pl.multiple_of(yy * CHUNK, CHUNK), CHUNK)
-        both = dot(q_eff[rows, :], terms, NT)
-        outputs = both[:, :HD] + both[:, HD:] + o_loc[rows, :]
-        scale = lax.rsqrt(jnp.mean(outputs * outputs, -1, keepdims=True) + 1e-05)
-        give[yy] = (outputs * scale * gain[...]).astype(BF16).reshape(2, ROWS, HD)
-        for cc in (c, other) if yy is not y else (other,):
-            remote(
-                give.at[yy, cc], got.at[h], give_send, got_recv.at[h], (s, head_of(yy, cc))
-            ).start()
+    both = dot(q_eff[...], terms, NT)
+    outputs = both[:, :HD] + both[:, HD:] + o_loc[...]
+    scale = lax.rsqrt(jnp.mean(outputs * outputs, -1, keepdims=True) + 1e-05)
+    give[...] = (outputs * scale * gain[...]).astype(BF16).reshape(Y_CHIPS, 2, ROWS, HD)
+    for yy, cc in (
+        (far, c), (far, other), (up, c), (down, c), (up, other), (down, other), (y, other)
+    ):
+        remote(
+            give.at[yy, cc], got.at[h], give_send, got_recv.at[h], (s, head_of(yy, cc))
+        ).start()
     got[h] = give[y, c]
     for yy in (y, up, down, far):
         arrived(outw.at[head_of(yy, other)], w_recv.at[yy, 2])

time: 56.1 us -> 54.5 us (0.971)
  Pallas kernels: 54.6 us -> 53.1 us
    pallas_call x1, Pallas kernels: 54.6 us -> 53.1 us  [local(): pl.pallas_call(functools.partial(layer, x_chips, z_chips), out_shape=jax....]
where the time goes in v6:
time: 54.5 us; the launch traced here: 54.4 us
  Pallas kernels  53.1 us (97%)
  local copies, waits for them, and re-layouts  0.66 us (1%)
  between operations  0.66 us (1%)
    pallas_call x1, Pallas kernels, local(): pl.pallas_call(functools.partial(layer, x_chips, z_chips), out_shape=jax....  53.1 us

profile of v6, /device:TPU:39, one launch (start us, length us, event | category | flops | bytes accessed | tf_op | source)
XLA Modules:
  0.0 54.4 jit_solution(12879451866495542145)
XLA Ops:
  0.7 53.1 %shard_map.91 = bf16[64,1024]{1,0:T(8,128)(2,1)S(1)} custom-call(bf16[64,1024]{1,0:T(8,128)(2,1)} %tok.1, bf16[1024,128]{1,0:T(8,128)(2,1)} %wq.1, bf16[1024,128]{1,0:T(8,128)(2,1)} %wk.1, bf16[1024,128]{1,0:T(8,128)(2,1)} %wv.1, bf16[1,1024]{1,0:T(2,128)(2,1)} %bitcast.2, f32[1]{0:T(128)S(6)} %copy.11.bias_in, f32[3,4,128]{2,1,0:T(4,128)} %conv_in.1, ...), custom_call_target="tpu_custom_call" | custom-call | tf_op jit(solution)/shard_map/pallas_call | solution.py:532
  53.7 0.7 %copy.12 = bf16[64,1024]{1,0:T(8,128)(2,1)} copy(bf16[64,1024]{1,0:T(8,128)(2,1)S(1)} %shard_map.91) | data formatting | bytes 262144

commit v7 on v6

--- a/solution.py
+++ b/solution.py
@@ -351,12 +351,17 @@
         return (x * z_chips + (z + z_chips + offset) % z_chips, h)
 
     duo[...] = before.astype(BF16)
-    to_even = remote(duo, mate, duo_send.at[0], duo_recv.at[0], at_z(-1))
+    tops, bottoms = pl.ds(0, HD), pl.ds(HD, HD)
+    to_even = [
+        remote(duo.at[rows], mate.at[rows], duo_send.at[0], duo_recv.at[2 * i], at_z(-1))
+        for i, rows in enumerate((tops, bottoms))
+    ]
     to_odd = remote(next_state, next_state, duo_send.at[1], duo_recv.at[1], at_z(1))
 
     @pl.when(odd == 1)
     def _():
-        to_even.start()
+        for copy in to_even:
+            copy.start()
 
     finish_outputs()
 
@@ -388,11 +393,21 @@
         for i in range(2):
             left[i] = lead
             right[i] = lead
-        arrived(mate, duo_recv.at[0])
-        own_f[...] = append(before, mate[...])
-        ring[j] = own_f[...].astype(BF16).reshape(SUBS, 2 * HD // SUBS, HD)
+        arrived(mate.at[tops], duo_recv.at[0])
+        product = twice(before, mate[tops])
+        own_f[tops] = product[:HD]
+        ring[j, pl.ds(0, HALF_SUBS)] = product[:HD].astype(BF16).reshape(HALF_SUBS, 2 * HD // SUBS, HD)
         if pairs == 8:
-            for q in range(SUBS):
+            for q in range(HALF_SUBS):
+                ring_copy(j, q, 2, q)
+                ring_copy(j, q, -2, q)
+        arrived(mate.at[bottoms], duo_recv.at[2])
+        own_f[bottoms] = product[HD:] + mate[bottoms].astype(F32)
+        ring[j, pl.ds(HALF_SUBS, HALF_SUBS)] = own_f[bottoms].astype(BF16).reshape(
+            HALF_SUBS, 2 * HD // SUBS, HD
+        )
+        if pairs == 8:
+            for q in range(HALF_SUBS, SUBS):
                 ring_copy(j, q, 2, q)
                 ring_copy(j, q, -2, q)
             for q in range(SUBS):
@@ -506,7 +521,7 @@
 
     @pl.when(odd == 1)
     def _():
-        to_even.wait_send()
+        settle(duo, duo_send.at[0])
 
     @pl.when(odd == 0)
     def _():
@@ -568,7 +583,7 @@
             dma,
             dma((Y_CHIPS, 3)),
             dma((2,)),
-            dma((2,)),
+            dma((3,)),
             dma,
             dma((z_chips // 2, SUBS)),
             dma,

time: 54.5 us -> 54.2 us (level)
  no operation moved by 1% of the time
where the time goes in v7:
time: 54.2 us; the launch traced here: 54 us
  Pallas kernels  52.6 us (97%)
  local copies, waits for them, and re-layouts  0.66 us (1%)
  between operations  0.66 us (1%)
    pallas_call x1, Pallas kernels, local(): pl.pallas_call(functools.partial(layer, x_chips, z_chips), out_shape=jax....  52.6 us

profile of v7, /device:TPU:39, one launch (start us, length us, event | category | flops | bytes accessed | tf_op | source)
XLA Modules:
  0.0 54.0 jit_solution(10806050585092604993)
XLA Ops:
  0.7 52.6 %shard_map.91 = bf16[64,1024]{1,0:T(8,128)(2,1)S(1)} custom-call(bf16[64,1024]{1,0:T(8,128)(2,1)} %tok.1, bf16[1024,128]{1,0:T(8,128)(2,1)} %wq.1, bf16[1024,128]{1,0:T(8,128)(2,1)} %wk.1, bf16[1024,128]{1,0:T(8,128)(2,1)} %wv.1, bf16[1,1024]{1,0:T(2,128)(2,1)} %bitcast.2, f32[1]{0:T(128)S(6)} %copy.11.bias_in, f32[3,4,128]{2,1,0:T(4,128)} %conv_in.1, ...), custom_call_target="tpu_custom_call" | custom-call | tf_op jit(solution)/shard_map/pallas_call | solution.py:547
  53.3 0.7 %copy.12 = bf16[64,1024]{1,0:T(8,128)(2,1)} copy(bf16[64,1024]{1,0:T(8,128)(2,1)S(1)} %shard_map.91) | data formatting | bytes 262144
